TPU v7x, 32 devices: a whole 2x2x4 slice. The times are simulated.
32 devices in a mesh: fsdp: 32 (over z, y, x, core).
Axes of the slice: x: 2, y: 2, z: 4, core: 2. Of those that a mesh axis runs over, the one named last changes fastest.
Arguments:
- hidden_in: bfloat16 [4096, 1024], P('fsdp'), may hold values from -6 to 6
- out_grad: bfloat16 [4096, 1024], P('fsdp'), may hold values from -6 to 6
- doc_ids: int32 [32, 128], P('fsdp'), may hold values from 0 to 3, never falling along the last dimension, each value on 1 to 64 neighbouring positions
- routes: int32 [4096, 6], P('fsdp'), may hold values from 0 to 63, all different within a row; in each aligned block of 128 rows (0 to 127, 128 to 255, ...) at most 16 rows name the same one
- gate_values: float32 [4096, 6], P('fsdp'), may hold values from 0.05 to 0.5
- attn_gain: bfloat16 [1024], P('fsdp'), may hold values from 0.5 to 1.5
- query_proj: bfloat16 [1024, 1536], P('fsdp'), may hold values from -0.1875 to 0.1875
- latent_proj: bfloat16 [1024, 576], P('fsdp'), may hold values from -0.1875 to 0.1875
- latent_gain: bfloat16 [512], P('fsdp'), may hold values from 0.5 to 1.5
- latent_up: bfloat16 [512, 2048], P('fsdp'), may hold values from -0.25 to 0.25
- output_proj: bfloat16 [1024, 1024], P('fsdp'), may hold values from -0.75 to 0.75
- ffn_gain: bfloat16 [1024], P('fsdp'), may hold values from 0.5 to 1.5
- shared_in: bfloat16 [1024, 2816], P('fsdp'), may hold values from -0.1875 to 0.1875
- shared_out: bfloat16 [1024, 1408], P('fsdp'), may hold values from -0.15625 to 0.15625
- expert_in: bfloat16 [128, 1024, 1408], P('fsdp'), may hold values from -0.1875 to 0.1875
- expert_out: bfloat16 [128, 704, 1024], P('fsdp'), may hold values from -0.21875 to 0.21875
Outputs:
- layer_out: bfloat16 [4096, 1024], P('fsdp')
- input_grad: float32 [4096, 1024], P('fsdp')
- grad_attn_gain: float32 [1024], P('fsdp')
- grad_query_proj: float32 [1024, 1536], P('fsdp')
- grad_latent_proj: float32 [1024, 576], P('fsdp')
- grad_latent_gain: float32 [512], P('fsdp')
- grad_latent_up: float32 [512, 2048], P('fsdp')
- grad_output_proj: float32 [1024, 1024], P('fsdp')
- grad_ffn_gain: float32 [1024], P('fsdp')
- grad_shared_in: float32 [1024, 2816], P('fsdp')
- grad_shared_out: float32 [1024, 1408], P('fsdp')
- grad_expert_in: float32 [128, 1024, 1408], P('fsdp')
- grad_expert_out: float32 [128, 704, 1024], P('fsdp')
Inputs may be any that keep to these rules, and one draw needn't show every extreme that they name: `doc_ids`: each row holds document numbers that never fall; each document is 1 to 64 positions long and one is exactly 64. `routes`: A token names 6 different experts. Among the tokens of one device no expert is named more than 16 times, a bound that some block reaches; every expert is named by some token.
All inputs are finite; a program needn't handle non-finite values.
Results may differ from a plain program's by a relative error of at most 0.014.
Values may be sent and summed in bfloat16 or wider, within the bound.
No kernel may reach another device: no remote copies, remote signals or barrier semaphores. Data moves between devices by JAX's collectives and lax.ppermute only.
A program may use at most 256 MiB of HBM per device.

v0:
```python
import math

import jax
import jax.numpy as jnp
from jax import lax
from jax.sharding import PartitionSpec as P

D = 1024
H = 8
NOPE = 128
ROPE = 64
VDIM = 128
RANK = 512
EXPERTS = 64
TOP = 6
CAP = 16


EPSILON = 1e-06


def matmul(left_side, right_side):
    return jnp.dot(left_side, right_side, preferred_element_type=jnp.float32)


def product(pattern, left_side, right_side):
    return jnp.einsum(pattern, left_side, right_side, preferred_element_type=jnp.float32)


def inverse_rms(values):
    return lax.rsqrt(jnp.mean(values * values, axis=-1, keepdims=True) + EPSILON)


def rotate(values, cosine_table, sine_table):
    middle = values.shape[-1] // 2
    first_half = values[..., :middle]
    second_half = values[..., middle:]
    return jnp.concatenate(
        [
            first_half * cosine_table - second_half * sine_table,
            second_half * cosine_table + first_half * sine_table,
        ],
        axis=-1,
    )


def unrotate(values, cosine_table, sine_table):
    middle = values.shape[-1] // 2
    first_half = values[..., :middle]
    second_half = values[..., middle:]
    return jnp.concatenate(
        [
            first_half * cosine_table + second_half * sine_table,
            second_half * cosine_table - first_half * sine_table,
        ],
        axis=-1,
    )


def swiglu_parts(pre_act):
    middle = pre_act.shape[-1] // 2
    gate_pre = pre_act[..., :middle]
    up_pre = pre_act[..., middle:]
    return (gate_pre, up_pre, jax.nn.sigmoid(gate_pre))


def swiglu_forward(pre_act):
    gate_pre, up_pre, sigmoid_gate = swiglu_parts(pre_act)
    return (gate_pre * sigmoid_gate * up_pre).astype(jnp.bfloat16)


def swiglu_backward(pre_act, grad_act):
    gate_pre, up_pre, sigmoid_gate = swiglu_parts(pre_act)
    silu_value = gate_pre * sigmoid_gate
    slope = sigmoid_gate * (1.0 + gate_pre * (1.0 - sigmoid_gate))
    return jnp.concatenate([grad_act * up_pre * slope, grad_act * silu_value], axis=-1).astype(
        jnp.bfloat16
    )


def prepare(query_raw, kv_raw, rope_key, documents):
    rows_here = query_raw.shape[0]
    indices = jnp.arange(rows_here, dtype=jnp.int32)
    same_doc = documents[:, None] == documents[None, :]
    starts = jnp.min(jnp.where(same_doc, indices[None, :], rows_here), axis=1)
    allowed = same_doc & (indices[None, :] <= indices[:, None])
    position = (indices - starts).astype(jnp.float32)
    frequency = jnp.exp(
        jnp.arange(ROPE // 2, dtype=jnp.float32) * (-2.0 * math.log(10000.0) / ROPE)
    )
    angles = position[:, None] * frequency[None, :]
    cosine_table = jnp.cos(angles)
    sine_table = jnp.sin(angles)
    query_heads = query_raw.reshape(rows_here, H, NOPE + ROPE)
    queries = jnp.concatenate(
        [
            query_heads[..., :NOPE],
            rotate(query_heads[..., NOPE:], cosine_table[:, None, :], sine_table[:, None, :]),
        ],
        axis=-1,
    ).astype(jnp.bfloat16)
    kv_heads = kv_raw.reshape(rows_here, H, NOPE + VDIM)
    turned = rotate(rope_key, cosine_table, sine_table)
    key_rows = jnp.concatenate(
        [kv_heads[..., :NOPE], jnp.broadcast_to(turned[:, None, :], (rows_here, H, ROPE))], axis=-1
    ).astype(jnp.bfloat16)
    value_rows = kv_heads[..., NOPE:].astype(jnp.bfloat16)
    return (queries, key_rows, value_rows, allowed, cosine_table, sine_table)


def attend(query_raw, kv_raw, rope_key, documents):
    queries, key_rows, value_rows, allowed, cosine_table, sine_table = prepare(
        query_raw, kv_raw, rope_key, documents
    )
    scaling = (NOPE + ROPE) ** (-0.5)
    scores = product("ihd,jhd->hij", queries, key_rows) * scaling
    log_total = jnp.log(jnp.sum(jnp.where(allowed[None], jnp.exp(scores), 0.0), axis=-1))
    rounded_probs = jnp.where(allowed[None], jnp.exp(scores - log_total[..., None]), 0.0).astype(
        jnp.bfloat16
    )
    head_out = product("hij,jhd->ihd", rounded_probs, value_rows).astype(jnp.bfloat16)
    return (head_out.reshape(head_out.shape[0], H * VDIM), log_total)


def attend_back(query_raw, kv_raw, rope_key, documents, log_total, head_out, grad_heads):
    queries, key_rows, value_rows, allowed, cosine_table, sine_table = prepare(
        query_raw, kv_raw, rope_key, documents
    )
    rows_here = query_raw.shape[0]
    scaling = (NOPE + ROPE) ** (-0.5)
    scores = product("ihd,jhd->hij", queries, key_rows) * scaling
    weights = jnp.where(allowed[None], jnp.exp(scores - log_total[..., None]), 0.0)
    rounded_probs = weights.astype(jnp.bfloat16)
    grad_three = grad_heads.reshape(rows_here, H, VDIM)
    heads_three = head_out.reshape(rows_here, H, VDIM)
    grad_probs = product("ihd,jhd->hij", grad_three, value_rows)
    deltas = jnp.sum(grad_three.astype(jnp.float32) * heads_three.astype(jnp.float32), axis=-1).T
    grad_scores = (weights * (grad_probs - deltas[..., None]) * scaling).astype(jnp.bfloat16)
    grad_queries = product("hij,jhd->ihd", grad_scores, key_rows)
    grad_keys = product("hij,ihd->jhd", grad_scores, queries)
    grad_values = product("hij,ihd->jhd", rounded_probs, grad_three)
    grad_query_raw = jnp.concatenate(
        [
            grad_queries[..., :NOPE],
            unrotate(grad_queries[..., NOPE:], cosine_table[:, None, :], sine_table[:, None, :]),
        ],
        axis=-1,
    ).reshape(rows_here, H * (NOPE + ROPE))
    grad_rope = unrotate(jnp.sum(grad_keys[..., NOPE:], axis=1), cosine_table, sine_table)
    grad_kv = jnp.concatenate([grad_keys[..., :NOPE], grad_values], axis=-1).reshape(
        rows_here, H * (NOPE + VDIM)
    )
    return (grad_query_raw, grad_kv, grad_rope)


def body(
    hidden_in,
    out_grad,
    doc_ids,
    routes,
    gate_values,
    attn_gain,
    query_proj,
    latent_proj,
    latent_gain,
    latent_up,
    output_proj,
    ffn_gain,
    shared_in,
    shared_out,
    expert_in,
    expert_out,
):
    full_attn_gain, full_query, full_latent, full_latent_gain, full_latent_up, full_output = (
        lax.all_gather(attn_gain, "fsdp", axis=0, tiled=True),
        lax.all_gather(query_proj, "fsdp", axis=0, tiled=True),
        lax.all_gather(latent_proj, "fsdp", axis=0, tiled=True),
        lax.all_gather(latent_gain, "fsdp", axis=0, tiled=True),
        lax.all_gather(latent_up, "fsdp", axis=0, tiled=True),
        lax.all_gather(output_proj, "fsdp", axis=0, tiled=True),
    )
    rows_here = hidden_in.shape[0]
    hidden_wide = hidden_in.astype(jnp.float32)
    scale_one = inverse_rms(hidden_wide)
    norm_one = hidden_wide * scale_one
    normed_one = (norm_one * full_attn_gain.astype(jnp.float32)).astype(jnp.bfloat16)
    query_raw = matmul(normed_one, full_query)
    latent_all = matmul(normed_one, full_latent)
    latent_part = latent_all[:, :RANK]
    rope_key = latent_all[:, RANK:]
    scale_latent = inverse_rms(latent_part)
    latent_norm = latent_part * scale_latent
    latent_in = (latent_norm * full_latent_gain.astype(jnp.float32)).astype(jnp.bfloat16)
    kv_raw = matmul(latent_in, full_latent_up)
    documents = doc_ids[0]
    head_out, log_total = attend(query_raw, kv_raw, rope_key, documents)
    mixed = hidden_wide + product("tv,dv->td", head_out, full_output)
    scale_two = inverse_rms(mixed)
    norm_two = mixed * scale_two
    full_ffn_gain, full_shared_in, full_shared_out = (
        lax.all_gather(ffn_gain, "fsdp", axis=0, tiled=True),
        lax.all_gather(shared_in, "fsdp", axis=0, tiled=True),
        lax.all_gather(shared_out, "fsdp", axis=0, tiled=True),
    )
    normed_two = (norm_two * full_ffn_gain.astype(jnp.float32)).astype(jnp.bfloat16)
    shared_pre = matmul(normed_two, full_shared_in)
    shared_act = swiglu_forward(shared_pre)
    shared_y = product("tf,df->td", shared_act, full_shared_out)
    devices = lax.axis_size("fsdp")
    per_device = expert_in.shape[0]
    flat_routes = routes.reshape(-1)
    chosen = (flat_routes[:, None] == jnp.arange(EXPERTS, dtype=jnp.int32)[None, :]).astype(
        jnp.int32
    )
    slot_index = jnp.sum((jnp.cumsum(chosen, axis=0) - chosen) * chosen, axis=1)
    piece_ids = flat_routes[:, None] * 2 + jnp.arange(2, dtype=jnp.int32)[None, :]
    target = piece_ids // per_device
    local_piece = piece_ids % per_device
    send_row = ((local_piece * devices + target) * CAP + slot_index[:, None]).reshape(-1)
    total_rows = 2 * EXPERTS * CAP
    owner_token = jnp.arange(send_row.shape[0], dtype=jnp.int32) // (2 * TOP)
    token_of_row = jnp.full((total_rows,), rows_here, dtype=jnp.int32).at[send_row].set(owner_token)
    gate_entries = jnp.repeat(gate_values.reshape(-1), 2)
    gate_rows = jnp.zeros((total_rows,), jnp.float32).at[send_row].set(gate_entries)
    selector = (token_of_row[:, None] == jnp.arange(rows_here, dtype=jnp.int32)[None, :]).astype(
        jnp.bfloat16
    )
    send_in = matmul(selector, normed_two).astype(jnp.bfloat16).reshape(per_device, devices, CAP, D)
    send_grad = (
        (gate_rows[:, None] * matmul(selector, out_grad))
        .astype(jnp.bfloat16)
        .reshape(per_device, devices, CAP, D)
    )
    got_in, got_grad = (
        lax.all_to_all(send_in, "fsdp", split_axis=1, concat_axis=1, tiled=True),
        lax.all_to_all(send_grad, "fsdp", split_axis=1, concat_axis=1, tiled=True),
    )
    piece_rows = got_in.reshape(per_device, devices * CAP, D)
    grad_rows = got_grad.reshape(per_device, devices * CAP, D)
    pre_act = product("prd,pdf->prf", piece_rows, expert_in)
    activation = swiglu_forward(pre_act)
    piece_out = product("prf,pfd->prd", activation, expert_out).astype(jnp.bfloat16)
    grad_act = product("prd,pfd->prf", grad_rows, expert_out)
    grad_expert_out = product("prf,prd->pfd", activation, grad_rows)
    grad_pre = swiglu_backward(pre_act, grad_act)
    grad_expert_in = product("prd,prf->pdf", piece_rows, grad_pre)
    piece_dx = product("prf,pdf->prd", grad_pre, expert_in).astype(jnp.bfloat16)
    back_out, back_dx = (
        lax.all_to_all(
            piece_out.reshape(per_device, devices, CAP, D),
            "fsdp",
            split_axis=1,
            concat_axis=1,
            tiled=True,
        ),
        lax.all_to_all(
            piece_dx.reshape(per_device, devices, CAP, D),
            "fsdp",
            split_axis=1,
            concat_axis=1,
            tiled=True,
        ),
    )
    routed_y = jnp.sum(
        (
            back_out.reshape(total_rows, D)[send_row].astype(jnp.float32) * gate_entries[:, None]
        ).reshape(rows_here, 2 * TOP, D),
        axis=1,
    )
    routed_dx = jnp.sum(
        back_dx.reshape(total_rows, D)[send_row].astype(jnp.float32).reshape(rows_here, 2 * TOP, D),
        axis=1,
    )
    layer_out = (mixed + shared_y + routed_y).astype(jnp.bfloat16)
    grad_shared_out = product("td,tf->df", out_grad, shared_act)
    grad_shared_act = matmul(out_grad, full_shared_out)
    grad_shared_pre = swiglu_backward(shared_pre, grad_shared_act)
    grad_shared_in = product("td,tf->df", normed_two, grad_shared_pre)
    grad_normed_two = product("tf,df->td", grad_shared_pre, full_shared_in) + routed_dx
    grad_ffn_gain = jnp.sum(grad_normed_two * norm_two, axis=0)
    grad_norm_two = grad_normed_two * full_ffn_gain.astype(jnp.float32)
    grad_mixed = out_grad.astype(jnp.float32) + scale_two * (
        grad_norm_two - norm_two * jnp.mean(grad_norm_two * norm_two, axis=-1, keepdims=True)
    )
    owned_ffn_gain, owned_shared_in, owned_shared_out = (
        lax.psum_scatter(grad_ffn_gain, "fsdp", scatter_dimension=0, tiled=True),
        lax.psum_scatter(grad_shared_in, "fsdp", scatter_dimension=0, tiled=True),
        lax.psum_scatter(grad_shared_out, "fsdp", scatter_dimension=0, tiled=True),
    )
    full_attn_gain, full_query, full_latent, full_latent_gain, full_latent_up, full_output = (
        lax.all_gather(attn_gain, "fsdp", axis=0, tiled=True),
        lax.all_gather(query_proj, "fsdp", axis=0, tiled=True),
        lax.all_gather(latent_proj, "fsdp", axis=0, tiled=True),
        lax.all_gather(latent_gain, "fsdp", axis=0, tiled=True),
        lax.all_gather(latent_up, "fsdp", axis=0, tiled=True),
        lax.all_gather(output_proj, "fsdp", axis=0, tiled=True),
    )
    mixed_low = grad_mixed.astype(jnp.bfloat16)
    grad_output_proj = product("td,tv->dv", mixed_low, head_out)
    grad_heads = matmul(mixed_low, full_output).astype(jnp.bfloat16)
    grad_query_wide, grad_kv_wide, grad_rope = attend_back(
        query_raw, kv_raw, rope_key, documents, log_total, head_out, grad_heads
    )
    grad_query_raw = grad_query_wide.astype(jnp.bfloat16)
    grad_kv = grad_kv_wide.astype(jnp.bfloat16)
    grad_latent_up = product("tr,tk->rk", latent_in, grad_kv)
    grad_latent_in = product("tk,rk->tr", grad_kv, full_latent_up)
    grad_latent_gain = jnp.sum(grad_latent_in * latent_norm, axis=0)
    grad_norm_latent = grad_latent_in * full_latent_gain.astype(jnp.float32)
    grad_latent = scale_latent * (
        grad_norm_latent
        - latent_norm * jnp.mean(grad_norm_latent * latent_norm, axis=-1, keepdims=True)
    )
    grad_latent_all = jnp.concatenate([grad_latent, grad_rope], axis=-1).astype(jnp.bfloat16)
    grad_query_proj = product("td,tq->dq", normed_one, grad_query_raw)
    grad_latent_proj = product("td,tq->dq", normed_one, grad_latent_all)
    grad_normed_one = product("tq,dq->td", grad_query_raw, full_query) + product(
        "tq,dq->td", grad_latent_all, full_latent
    )
    grad_attn_gain = jnp.sum(grad_normed_one * norm_one, axis=0)
    grad_norm_one = grad_normed_one * full_attn_gain.astype(jnp.float32)
    input_grad = grad_mixed + scale_one * (
        grad_norm_one - norm_one * jnp.mean(grad_norm_one * norm_one, axis=-1, keepdims=True)
    )
    owned_attn_gain, owned_query, owned_latent, owned_latent_gain, owned_latent_up, owned_output = (
        lax.psum_scatter(grad_attn_gain, "fsdp", scatter_dimension=0, tiled=True),
        lax.psum_scatter(grad_query_proj, "fsdp", scatter_dimension=0, tiled=True),
        lax.psum_scatter(grad_latent_proj, "fsdp", scatter_dimension=0, tiled=True),
        lax.psum_scatter(grad_latent_gain, "fsdp", scatter_dimension=0, tiled=True),
        lax.psum_scatter(grad_latent_up, "fsdp", scatter_dimension=0, tiled=True),
        lax.psum_scatter(grad_output_proj, "fsdp", scatter_dimension=0, tiled=True),
    )
    return (
        layer_out,
        input_grad,
        owned_attn_gain,
        owned_query,
        owned_latent,
        owned_latent_gain,
        owned_latent_up,
        owned_output,
        owned_ffn_gain,
        owned_shared_in,
        owned_shared_out,
        grad_expert_in,
        grad_expert_out,
    )


def solution(mesh):
    in_specs = (
        P("fsdp", None),
        P("fsdp", None),
        P("fsdp", None),
        P("fsdp", None),
        P("fsdp", None),
        P("fsdp"),
        P("fsdp", None),
        P("fsdp", None),
        P("fsdp"),
        P("fsdp", None),
        P("fsdp", None),
        P("fsdp"),
        P("fsdp", None),
        P("fsdp", None),
        P("fsdp", None, None),
        P("fsdp", None, None),
    )
    out_specs = (
        P("fsdp", None),
        P("fsdp", None),
        P("fsdp"),
        P("fsdp", None),
        P("fsdp", None),
        P("fsdp"),
        P("fsdp", None),
        P("fsdp", None),
        P("fsdp"),
        P("fsdp", None),
        P("fsdp", None),
        P("fsdp", None, None),
        P("fsdp", None, None),
    )
    return jax.shard_map(body, mesh=mesh, in_specs=in_specs, out_specs=out_specs, check_vma=False)
```

profile of v0, /device:TPU:0, one launch (start us, length us, event | category | flops | bytes accessed | tf_op | source)
XLA Modules:
  0.0 1393.0 jit_solution(18309700321392656517)
XLA Ops:
  16.2 6.2 scatter_custom_fusion
  22.4 6.2 scatter_custom_fusion.1
  32.6 7.5 all-to-all-start.2
  40.8 127.8 %all-reduce.7 = (bf16[1024]{0:T(1024)(128)(2,1)S(1)}, bf16[512]{0:T(512)(128)(2,1)S(1)}, bf16[1024]{0:T(1024)(128)(2,1)S(1)}) all-reduce(bf16[1024]{0:T(1024)(128)(2,1)S(1)} %dynamic-update-slice, bf16[512]{0:T(512)(128)(2,1)S(1)} %dynamic-update-slice.1, bf16[1024]{0:T(1024)(128)(2,1)S(1)} %dynamic-update-slice.2), channel_id=1, replica_groups=mesh['fsdp'=32] {'fsdp'}, use_global_device_ids=true, to_apply=%add | all-reduce | flops 2560 | bytes 10240
  174.0 38.4 %all-gather.11.cloned.1.call-done = bf16[1024,1536]{1,0:T(8,128)(2,1)} async-done(((bf16[32,1536]{1,0:T(8,128)(2,1)}), bf16[1024,1536]{1,0:T(8,128)(2,1)}) %all-gather.11.cloned.1.call-update) | async-done | bytes 3145744 | tf_op jit(solution)/shard_map/all_gather | solution.py:176
  212.4 3.3 fusion.88
  217.1 52.9 %all-gather.13.cloned.1.call-done = bf16[1024,1024]{1,0:T(8,128)(2,1)} async-done(((bf16[32,1024]{1,0:T(8,128)(2,1)}), bf16[1024,1024]{1,0:T(8,128)(2,1)}) %all-gather.13.cloned.1.call-update) | async-done | bytes 2097168 | tf_op jit(solution)/shard_map/all_gather | solution.py:180
  276.7 3.6 all-to-all-start
  280.9 5.0 copy.123
  285.9 97.5 %all-gather.15.cloned.1.call-done = bf16[1024,2816]{1,0:T(8,128)(2,1)} async-done(((bf16[32,2816]{1,0:T(8,128)(2,1)}), bf16[1024,2816]{1,0:T(8,128)(2,1)}) %all-gather.15.cloned.1.call-update) | async-done | bytes 5767184 | tf_op jit(solution)/shard_map/all_gather | solution.py:202
  383.5 4.7 fusion.92
  388.1 56.9 %all-gather.17.cloned.1.call-done = bf16[1024,1408]{1,0:T(8,128)(2,1)} async-done(((bf16[32,1408]{1,0:T(8,128)(2,1)}), bf16[1024,1408]{1,0:T(8,128)(2,1)}) %all-gather.17.cloned.1.call-update) | async-done | bytes 2883600 | tf_op jit(solution)/shard_map/all_gather | solution.py:203
  445.1 3.8 multiply_convert_fusion.5
  448.9 5.1 copy.115
  453.9 15.8 %fusion.93 = f32[4,512,1408]{1,2,0:T(8,128)} fusion(bf16[4,512,1024]{2,1,0:T(8,128)(2,1)} %bitcast.97, bf16[4,1024,1408]{2,1,0:T(8,128)(2,1)} %param.30), kind=kOutput, calls=%fused_computation.179 | convolution fusion | flops 5905580032 | bytes 27262976 | tf_op jit(solution)/shard_map/prd,pdf->prf/dot_general | solution.py:27
  469.8 12.4 multiply_convert_fusion.2
  482.2 13.8 fusion.4
  496.0 5.0 copy.125
  501.0 3.6 all-to-all-start.3
  504.7 3.5 convolution_bitcast_fusion
  508.2 6.4 copy.152
  515.6 96.7 %all-to-all-done.3 = bf16[4,32,16,1024]{3,2,0,1:T(8,128)(2,1)} async-done(((bf16[4,32,16,1024]{3,2,0,1:T(8,128)(2,1)}), bf16[4,32,16,1024]{3,2,0,1:T(8,128)(2,1)}, u32[]{:S(2)}, u32[]{:S(2)}) %all-to-all-start.3) | async-done | bytes 4194336 | tf_op jit(solution)/shard_map/all_to_all | solution.py:256
  612.3 5.1 copy.126
  617.4 10.6 gather_fusion.1
  628.0 6.4 reshape.395
  634.4 5.5 reduce_sum.141
  639.9 5.7 multiply_reduce_fusion.1
  653.4 3.0 multiply_reduce_fusion.5
  657.3 2.8 fusion.45
  662.2 4.4 fusion.86
  666.8 3.3 fusion.84
  670.1 2.7 fusion.39
  673.1 7.0 fusion.30
  680.2 7.0 convolution_convert_fusion.1
  689.7 6.4 all-to-all-start.1
  696.3 10.7 fusion.95
  707.0 15.2 %fusion.2 = f32[4,1024,1408]{2,1,0:T(8,128)} fusion(bf16[4,512,1024]{2,1,0:T(8,128)(2,1)} %bitcast.98, bf16[4,512,704]{1,2,0:T(8,128)(2,1)} %get-tuple-element.78, bf16[4,512,704]{1,2,0:T(8,128)(2,1)} %get-tuple-element.77), kind=kOutput, calls=%fused_computation.15 | convolution fusion | flops 5917114368 | bytes 33030144 | tf_op jit(solution)/shard_map/prd,prf->pdf/dot_general | solution.py:27
  722.2 75.6 %all-to-all-done.1 = bf16[4,32,16,1024]{3,2,0,1:T(8,128)(2,1)} async-done(((bf16[4,32,16,1024]{3,2,0,1:T(8,128)(2,1)}), bf16[4,32,16,1024]{3,2,0,1:T(8,128)(2,1)}, u32[]{:S(2)}, u32[]{:S(2)}) %all-to-all-start.1) | async-done | bytes 4194336 | tf_op jit(solution)/shard_map/all_to_all | solution.py:249
  797.8 5.1 copy.119
  802.9 10.5 gather_fusion
  813.4 6.5 reshape.394
  819.9 3.1 fusion.94
  823.8 39.5 %all-reduce.6 = (f32[1024]{0:T(1024)S(1)}, f32[512]{0:T(512)S(1)}, f32[1024]{0:T(1024)S(1)}) all-reduce(f32[1024]{0:T(1024)S(1)} %get-tuple-element.67, f32[512]{0:T(512)S(1)} %copy-done.21, f32[1024]{0:T(1024)S(1)} %copy-done.18), channel_id=2, replica_groups=mesh['fsdp'=32] {'fsdp'}, use_global_device_ids=true, to_apply=%region_18.19.clone | all-reduce | flops 2560 | bytes 20480
  866.1 5.5 multiply_reduce_fusion
  873.4 70.8 %reduce-scatter.9.cloned.1.call-done = f32[32,1536]{1,0:T(8,128)} async-done(((f32[1024,1536]{1,0:T(8,128)}), f32[32,1536]{1,0:T(8,128)}) %reduce-scatter.9.cloned.1.call-update) | async-done | bytes 196624 | tf_op jit(solution)/shard_map/reduce_scatter | solution.py:327
  944.3 144.9 %reduce-scatter.13.cloned.1.call-done = f32[16,2048]{1,0:T(8,128)} async-done(((f32[512,2048]{1,0:T(8,128)}), f32[16,2048]{1,0:T(8,128)}) %reduce-scatter.13.cloned.1.call-update) | async-done | bytes 131088 | tf_op jit(solution)/shard_map/reduce_scatter | solution.py:330
  1089.1 141.5 %reduce-scatter.15.cloned.1.call-done = f32[32,1024]{1,0:T(8,128)} async-done(((f32[1024,1024]{1,0:T(8,128)}), f32[32,1024]{1,0:T(8,128)}) %reduce-scatter.15.cloned.1.call-update) | async-done | bytes 131088 | tf_op jit(solution)/shard_map/reduce_scatter | solution.py:331
  1230.6 155.1 %reduce-scatter.17.cloned.1.call-done = f32[32,2816]{1,0:T(8,128)} async-done(((f32[1024,2816]{1,0:T(8,128)}), f32[32,2816]{1,0:T(8,128)}) %reduce-scatter.17.cloned.1.call-update) | async-done | bytes 360464 | tf_op jit(solution)/shard_map/reduce_scatter | solution.py:287
  (182 shorter events, 47.4 us)
Async XLA Ops:
  7.2 21.4 %copy-start.4 = (bf16[128,1024]{1,0:T(8,128)(2,1)S(1)}, bf16[128,1024]{1,0:T(8,128)(2,1)}, u32[]{:S(2)}) copy-start(bf16[128,1024]{1,0:T(8,128)(2,1)} %param.17) | copy-start | bytes 786436
  7.2 162.1 %all-gather.7.cloned.1.call-start = ((), (), s32[]{:S(2)}) async-start(), calls=%async_computation.10 | async-start | bytes 1351680 | tf_op jit(solution)/shard_map/all_gather | solution.py:177
  7.9 163.6 %all-gather.9.cloned.1.call-start = ((), (), s32[]{:S(2)}) async-start(), calls=%async_computation.11 | async-start | bytes 2162688 | tf_op jit(solution)/shard_map/all_gather | solution.py:179
  8.7 203.7 %all-gather.11.cloned.1.call-start = ((), (), s32[]{:S(2)}) async-start(), calls=%async_computation.12 | async-start | bytes 3244032 | tf_op jit(solution)/shard_map/all_gather | solution.py:176
  9.4 260.7 %all-gather.13.cloned.1.call-start = ((), (), s32[]{:S(2)}) async-start(), calls=%async_computation.13 | async-start | bytes 2162688 | tf_op jit(solution)/shard_map/all_gather | solution.py:180
  10.0 373.5 %all-gather.15.cloned.1.call-start = ((), (), s32[]{:S(2)}) async-start(), calls=%async_computation.14 | async-start | bytes 5947392 | tf_op jit(solution)/shard_map/all_gather | solution.py:202
  32.6 7.5 copy-start.29
  32.6 7.7 copy-start.30
  32.6 8.0 copy-start.31
  32.6 136.1 %copy-start.28 = (s32[1,128]{1,0:T(1,128)S(1)}, s32[1,128]{1,0:T(1,128)}, u32[]{:S(2)}) copy-start(s32[1,128]{1,0:T(1,128)} %param.18) | copy-start | bytes 1540
  32.6 136.2 %copy-start = (bf16[128,1024]{1,0:T(8,128)(2,1)S(1)}, bf16[128,1024]{1,0:T(8,128)(2,1)}, u32[]{:S(2)}) copy-start(bf16[128,1024]{1,0:T(8,128)(2,1)} %param.16) | copy-start | bytes 786436
  32.6 244.1 %all-to-all-start.2 = ((bf16[4,32,16,1024]{3,2,0,1:T(8,128)(2,1)}), bf16[4,32,16,1024]{3,2,0,1:T(8,128)(2,1)}, u32[]{:S(2)}, u32[]{:S(2)}) async-start(bf16[4,32,16,1024]{3,2,0,1:T(8,128)(2,1)} %copy.122), calls=%async_computation.2 | async-start | bytes 8388608 | tf_op jit(solution)/shard_map/all_to_all | solution.py:236
  168.7 2.7 copy-start.24
  169.0 46.7 %copy-start.16 = (f32[128]{0:T(128)}, f32[128]{0:T(128)S(1)}, u32[]{:S(2)}) copy-start(f32[128]{0:T(128)S(1)} %add_rsqrt_fusion.2) | copy-start | bytes 1540
  169.0 2.4 copy-start.26
  169.1 345.5 %copy-start.20 = (pred[128,128]{0,1:T(8,128)(4,1)}, pred[128,128]{0,1:T(8,128)(4,1)S(1)}, u32[]{:S(2)}) copy-start(pred[128,128]{0,1:T(8,128)(4,1)S(1)} %compare_and_fusion) | copy-start | bytes 49156
  169.2 46.5 %copy-start.10 = (f32[128,32]{0,1:T(8,128)}, f32[128,32]{0,1:T(8,128)S(1)}, u32[]{:S(2)}) copy-start(f32[128,32]{0,1:T(8,128)S(1)} %get-tuple-element.91) | copy-start | bytes 49156
  169.2 46.5 %copy-start.11 = (f32[128,32]{0,1:T(8,128)}, f32[128,32]{0,1:T(8,128)S(1)}, u32[]{:S(2)}) copy-start(f32[128,32]{0,1:T(8,128)S(1)} %get-tuple-element.92) | copy-start | bytes 49156
  171.5 44.1 %copy-start.22 = (f32[128]{0:T(128)}, f32[128]{0:T(128)S(1)}, u32[]{:S(2)}) copy-start(f32[128]{0:T(128)S(1)} %add_rsqrt_fusion.1) | copy-start | bytes 1540
  174.0 43.1 %copy-start.5 = (bf16[128,2048]{0,1:T(8,128)(2,1)}, bf16[128,2048]{0,1:T(8,128)(2,1)S(1)}, u32[]{:S(2)}) copy-start(bf16[128,2048]{0,1:T(8,128)(2,1)S(1)} %copy.154) | copy-start | bytes 1572868
  174.0 43.1 %copy-start.7 = (bf16[128,8,128]{0,2,1:T(8,128)(2,1)}, bf16[128,8,128]{0,2,1:T(8,128)(2,1)S(1)}, u32[]{:S(2)}) copy-start(bf16[128,8,128]{0,2,1:T(8,128)(2,1)S(1)} %slice.119) | copy-start | bytes 786436
  215.8 58.5 %copy-start.9 = (bf16[128,8,32]{0,2,1:T(8,128)(2,1)}, bf16[128,8,32]{0,2,1:T(8,128)(2,1)S(1)}, u32[]{:S(2)}) copy-start(bf16[128,8,32]{0,2,1:T(8,128)(2,1)S(1)} %get-tuple-element.86) | copy-start | bytes 196612
  216.8 297.9 %copy-start.32 = (f32[8,128,128]{1,2,0:T(8,128)}, f32[8,128,128]{1,2,0:T(8,128)S(1)}, u32[]{:S(2)}) copy-start(f32[8,128,128]{1,2,0:T(8,128)S(1)} %convolution_multiply_fusion) | copy-start | bytes 1572868
  276.7 172.2 %all-to-all-start = ((bf16[4,32,16,1024]{3,2,0,1:T(8,128)(2,1)}), bf16[4,32,16,1024]{3,2,0,1:T(8,128)(2,1)}, u32[]{:S(2)}, u32[]{:S(2)}) async-start(bf16[4,32,16,1024]{3,2,0,1:T(8,128)(2,1)} %copy.114), calls=%async_computation | async-start | bytes 8388608 | tf_op jit(solution)/shard_map/all_to_all | solution.py:235
  280.3 164.8 %all-gather.17.cloned.1.call-start = ((), (), s32[]{:S(2)}) async-start(), calls=%async_computation.15 | async-start | bytes 2973696 | tf_op jit(solution)/shard_map/all_gather | solution.py:203
  501.0 111.3 %all-to-all-start.3 = ((bf16[4,32,16,1024]{3,2,0,1:T(8,128)(2,1)}), bf16[4,32,16,1024]{3,2,0,1:T(8,128)(2,1)}, u32[]{:S(2)}, u32[]{:S(2)}) async-start(bf16[4,32,16,1024]{3,2,0,1:T(8,128)(2,1)} %copy.125), calls=%async_computation.3 | async-start | bytes 8388608 | tf_op jit(solution)/shard_map/all_to_all | solution.py:256
  504.6 368.8 %reduce-scatter.19.cloned.1.call-start = ((), (), s32[]{:S(2)}) async-start(), calls=%async_computation.21 | async-start | bytes 5947392
  514.6 358.9 %reduce-scatter.11.cloned.1.call-start = ((), (), s32[]{:S(2)}) async-start(), calls=%async_computation.17 | async-start | bytes 2703360 | tf_op jit(solution)/shard_map/reduce_scatter | solution.py:328
  514.6 102.7 %copy-start.14 = (s32[2048]{0:T(1024)}, s32[2048]{0:T(1024)S(1)}, u32[]{:S(2)}) copy-start(s32[2048]{0:T(1024)S(1)} %pad_clamp_fusion) | copy-start | bytes 24580
  639.8 6.0 copy-start.1
  645.8 7.6 copy-start.23
  646.5 9.9 copy-start.25
  646.6 9.9 copy-start.27
  656.6 0.7 copy-start.12
  660.1 284.2 %reduce-scatter.9.cloned.1.call-start = ((), (), s32[]{:S(2)}) async-start(), calls=%async_computation.16 | async-start | bytes 6488064 | tf_op jit(solution)/shard_map/reduce_scatter | solution.py:327
  666.7 422.4 %reduce-scatter.13.cloned.1.call-start = ((), (), s32[]{:S(2)}) async-start(), calls=%async_computation.18 | async-start | bytes 4325376 | tf_op jit(solution)/shard_map/reduce_scatter | solution.py:330
  670.1 3.1 copy-start.6
  670.1 560.5 %reduce-scatter.15.cloned.1.call-start = ((), (), s32[]{:S(2)}) async-start(), calls=%async_computation.19 | async-start | bytes 4325376 | tf_op jit(solution)/shard_map/reduce_scatter | solution.py:331
  672.9 712.8 %reduce-scatter.17.cloned.1.call-start = ((), (), s32[]{:S(2)}) async-start(), calls=%async_computation.20 | async-start | bytes 11894784 | tf_op jit(solution)/shard_map/reduce_scatter | solution.py:287
  689.7 6.4 copy-start.19
  689.7 108.1 %all-to-all-start.1 = ((bf16[4,32,16,1024]{3,2,0,1:T(8,128)(2,1)}), bf16[4,32,16,1024]{3,2,0,1:T(8,128)(2,1)}, u32[]{:S(2)}, u32[]{:S(2)}) async-start(bf16[4,32,16,1024]{3,2,0,1:T(8,128)(2,1)} %copy.118), calls=%async_computation.1 | async-start | bytes 8388608 | tf_op jit(solution)/shard_map/all_to_all | solution.py:249
  722.2 80.7 %copy-start.15 = (s32[2048]{0:T(1024)S(1)}, s32[2048]{0:T(1024)}, u32[]{:S(2)}) copy-start(s32[2048]{0:T(1024)} %copy-done.14) | copy-start | bytes 24580
  813.4 9.7 copy-start.13
  813.4 9.7 copy-start.17
  819.9 3.2 copy-start.2
  819.9 3.9 copy-start.18
  819.9 3.9 copy-start.21
  866.1 5.6 copy-start.3
  (1 other events, 0.7 us)
Sparse Core Ops, SparseCore 0:
  10.9 71.0 all-gather.6
  84.8 66.1 all-gather.8
  153.8 58.5 all-gather.10
  215.1 54.9 all-gather.12
  272.7 110.6 all-gather.14
  386.2 58.8 all-gather.16
  514.7 162.2 reduce-scatter.18
  679.8 147.2 reduce-scatter.10
  833.3 110.9 reduce-scatter.8
  947.0 142.1 reduce-scatter.12
  1092.0 138.5 reduce-scatter.14
  1233.3 152.2 reduce-scatter.16
where the time goes:
time: 1400 us; the launch traced here: 1390 us
  waiting for transfers between devices  934 us (67%)
  blocking collectives  167 us (12%)
  matrix products  142 us (10%)
  local copies, waits for them, and re-layouts  93.3 us (7%)
  starting transfers between devices  21.8 us (2%)
  other arithmetic  19.2 us (1%)
  between operations  15.5 us (1%)
    unnamed x2, blocking collectives  167 us
    reduce_scatter x1, waiting for transfers between devices, body(): lax.psum_scatter(grad_shared_in, 'fsdp', scatter_dimension=0, tiled=True)  155 us
    reduce_scatter x1, waiting for transfers between devices, body(): lax.psum_scatter(grad_latent_up, 'fsdp', scatter_dimension=0, tiled=True)  145 us
    reduce_scatter x1, waiting for transfers between devices, body(): lax.psum_scatter(grad_output_proj, 'fsdp', scatter_dimension=0, tiled=True)  141 us
    dot_general x24, matrix products, product(): jnp.einsum(pattern, left_side, right_side, preferred_element_type=jnp.flo...  122 us
    all_gather x1, waiting for transfers between devices, body(): lax.all_gather(shared_in, 'fsdp', axis=0, tiled=True)  97.5 us
    all_to_all x1, waiting for transfers between devices, body(): lax.all_to_all(piece_dx.reshape(per_device, devices, CAP, D), 'fsdp', spl...  96.7 us
    all_to_all x1, waiting for transfers between devices, body(): lax.all_to_all(piece_out.reshape(per_device, devices, CAP, D), 'fsdp', sp...  75.6 us
  transfers between devices with their start and end apart: 16, of which 10 were waited for; matrix products, arithmetic and copies ran while one was open for 14% of the time, Pallas kernels for 0%

commit v1 on v0

v1 whole, which is shorter than its diff:
```python
import math

import jax
import jax.numpy as jnp
from jax import lax
from jax.sharding import PartitionSpec as P

D = 1024
H = 8
NOPE = 128
ROPE = 64
VDIM = 128
RANK = 512
EXPERTS = 64
TOP = 6
CAP = 16
QW = H * (NOPE + ROPE)
OW = H * VDIM
UW = H * (NOPE + VDIM) // 2
LW = RANK + ROPE
ATT_W = 4224

EPSILON = 1e-06
F32 = jnp.float32
BF16 = jnp.bfloat16


def matmul(left_side, right_side):
    return jnp.dot(left_side, right_side, preferred_element_type=F32)


def product(pattern, left_side, right_side):
    return jnp.einsum(pattern, left_side, right_side, preferred_element_type=F32)


def inverse_rms(values):
    return lax.rsqrt(jnp.mean(values * values, axis=-1, keepdims=True) + EPSILON)


def rotate(values, cosine_table, sine_table):
    middle = values.shape[-1] // 2
    first_half = values[..., :middle]
    second_half = values[..., middle:]
    return jnp.concatenate(
        [
            first_half * cosine_table - second_half * sine_table,
            second_half * cosine_table + first_half * sine_table,
        ],
        axis=-1,
    )


def unrotate(values, cosine_table, sine_table):
    return rotate(values, cosine_table, -sine_table)


def swiglu_parts(pre_act):
    middle = pre_act.shape[-1] // 2
    gate_pre = pre_act[..., :middle]
    up_pre = pre_act[..., middle:]
    return (gate_pre, up_pre, jax.nn.sigmoid(gate_pre))


def swiglu_forward(pre_act):
    gate_pre, up_pre, sigmoid_gate = swiglu_parts(pre_act)
    return (gate_pre * sigmoid_gate * up_pre).astype(BF16)


def swiglu_backward(pre_act, grad_act):
    gate_pre, up_pre, sigmoid_gate = swiglu_parts(pre_act)
    silu_value = gate_pre * sigmoid_gate
    slope = sigmoid_gate * (1.0 + gate_pre * (1.0 - sigmoid_gate))
    return jnp.concatenate([grad_act * up_pre * slope, grad_act * silu_value], axis=-1).astype(BF16)


def tables(documents):
    rows_here = documents.shape[0]
    indices = jnp.arange(rows_here, dtype=jnp.int32)
    same_doc = documents[:, None] == documents[None, :]
    starts = jnp.min(jnp.where(same_doc, indices[None, :], rows_here), axis=1)
    allowed = same_doc & (indices[None, :] <= indices[:, None])
    position = (indices - starts).astype(F32)
    frequency = jnp.exp(jnp.arange(ROPE // 2, dtype=F32) * (-2.0 * math.log(10000.0) / ROPE))
    angles = position[:, None] * frequency[None, :]
    return (allowed, jnp.cos(angles), jnp.sin(angles))


def prepare(query_raw, kv_raw, rope_key, cosine_table, sine_table):
    rows_here = query_raw.shape[0]
    query_heads = query_raw.reshape(rows_here, H, NOPE + ROPE)
    queries = jnp.concatenate(
        [
            query_heads[..., :NOPE],
            rotate(query_heads[..., NOPE:], cosine_table[:, None, :], sine_table[:, None, :]),
        ],
        axis=-1,
    ).astype(BF16)
    kv_heads = kv_raw.reshape(rows_here, H, NOPE + VDIM)
    turned = rotate(rope_key, cosine_table, sine_table)
    key_rows = jnp.concatenate(
        [kv_heads[..., :NOPE], jnp.broadcast_to(turned[:, None, :], (rows_here, H, ROPE))], axis=-1
    ).astype(BF16)
    value_rows = kv_heads[..., NOPE:].astype(BF16)
    return (queries, key_rows, value_rows)


def attend(queries, key_rows, value_rows, allowed):
    scaling = (NOPE + ROPE) ** (-0.5)
    scores = product("ihd,jhd->hij", queries, key_rows) * scaling
    log_total = jnp.log(jnp.sum(jnp.where(allowed[None], jnp.exp(scores), 0.0), axis=-1))
    weights = jnp.where(allowed[None], jnp.exp(scores - log_total[..., None]), 0.0)
    head_out = product("hij,jhd->ihd", weights.astype(BF16), value_rows).astype(BF16)
    return (head_out.reshape(head_out.shape[0], H * VDIM), weights)


def attend_back(queries, key_rows, value_rows, weights, cosine_table, sine_table, head_out, grad_heads):
    rows_here = queries.shape[0]
    scaling = (NOPE + ROPE) ** (-0.5)
    rounded_probs = weights.astype(BF16)
    grad_three = grad_heads.reshape(rows_here, H, VDIM)
    heads_three = head_out.reshape(rows_here, H, VDIM)
    grad_probs = product("ihd,jhd->hij", grad_three, value_rows)
    deltas = jnp.sum(grad_three.astype(F32) * heads_three.astype(F32), axis=-1).T
    grad_scores = (weights * (grad_probs - deltas[..., None]) * scaling).astype(BF16)
    grad_queries = product("hij,jhd->ihd", grad_scores, key_rows)
    grad_keys = product("hij,ihd->jhd", grad_scores, queries)
    grad_values = product("hij,ihd->jhd", rounded_probs, grad_three)
    grad_query_raw = jnp.concatenate(
        [
            grad_queries[..., :NOPE],
            unrotate(grad_queries[..., NOPE:], cosine_table[:, None, :], sine_table[:, None, :]),
        ],
        axis=-1,
    ).reshape(rows_here, H * (NOPE + ROPE))
    grad_rope = unrotate(jnp.sum(grad_keys[..., NOPE:], axis=1), cosine_table, sine_table)
    grad_kv = jnp.concatenate([grad_keys[..., :NOPE], grad_values], axis=-1).reshape(
        rows_here, H * (NOPE + VDIM)
    )
    return (grad_query_raw, grad_kv, grad_rope)


def body(
    hidden_in,
    out_grad,
    doc_ids,
    routes,
    gate_values,
    attn_gain,
    query_proj,
    latent_proj,
    latent_gain,
    latent_up,
    output_proj,
    ffn_gain,
    shared_in,
    shared_out,
    expert_in,
    expert_out,
):
    devices = lax.axis_size("fsdp")
    rows_here = hidden_in.shape[0]
    own = D // devices
    half = own // 2

    gains = jnp.concatenate(
        [
            attn_gain[:, None],
            ffn_gain[:, None],
            jnp.concatenate([latent_gain, jnp.zeros_like(latent_gain)])[:, None],
            jnp.zeros((own, ATT_W - QW - OW - UW - LW - 3), BF16),
        ],
        axis=1,
    )
    packed = jnp.concatenate(
        [
            query_proj,
            output_proj,
            jnp.concatenate([latent_up[:, :UW], latent_up[:, UW:]], axis=0),
            latent_proj,
            gains,
        ],
        axis=1,
    )
    gathered = lax.all_gather(packed, "fsdp", axis=0, tiled=True)
    gathered_shared = lax.all_gather(
        jnp.concatenate([shared_in, shared_out], axis=1), "fsdp", axis=0, tiled=True
    )

    per_device = expert_in.shape[0]
    pieces = 2 if per_device % 2 == 0 else 1
    units = 2 * EXPERTS // pieces
    local_units = units // devices
    unit_expert = jnp.arange(units, dtype=jnp.int32) // (2 // pieces)
    named = routes[:, :, None] == unit_expert[None, None, :]
    hits = jnp.any(named, axis=1)
    gates = jnp.sum(jnp.where(named, gate_values[:, :, None], 0.0), axis=1)
    token = jnp.arange(rows_here, dtype=jnp.int32)
    earlier = (token[None, :] < token[:, None]).astype(BF16)
    slots = matmul(earlier, hits.astype(BF16)).astype(jnp.int32)
    slots = jnp.where(hits, slots, CAP)
    by_row = lambda table: table.T.reshape(devices, local_units, rows_here).transpose(1, 0, 2)
    row_slots = by_row(slots)
    row_gates = by_row(gates)
    chosen = row_slots[:, :, None, :] == jnp.arange(CAP, dtype=jnp.int32)[None, None, :, None]
    selector = chosen.astype(BF16).reshape(local_units, devices * CAP, rows_here)
    gate_wide = jnp.where(chosen, row_gates[:, :, None, :], 0.0).reshape(
        local_units, devices * CAP, rows_here
    )
    gate_rows = jnp.sum(gate_wide, axis=-1, keepdims=True)

    def exchange(rows):
        return lax.all_to_all(
            rows.reshape(devices, CAP, D), "fsdp", split_axis=0, concat_axis=0, tiled=True
        ).reshape(devices * CAP, D)

    grad_rows = [
        exchange((gate_rows[u] * matmul(selector[u], out_grad)).astype(BF16))
        for u in range(local_units)
    ]

    full_query = gathered[:, :QW]
    full_output = gathered[:, QW : QW + OW]
    ups = gathered[:, QW + OW : QW + OW + UW].reshape(devices, 2, half, UW)
    up_left = ups[:, 0].reshape(RANK, UW)
    up_right = ups[:, 1].reshape(RANK, UW)
    full_latent = gathered[:, QW + OW + UW : QW + OW + UW + LW]
    gain_at = QW + OW + UW + LW
    full_attn_gain = gathered[:, gain_at].astype(F32)
    full_ffn_gain = gathered[:, gain_at + 1].astype(F32)
    full_latent_gain = (
        gathered[:, gain_at + 2].reshape(devices, own)[:, :half].reshape(RANK).astype(F32)
    )

    hidden_wide = hidden_in.astype(F32)
    scale_one = inverse_rms(hidden_wide)
    norm_one = hidden_wide * scale_one
    normed_one = (norm_one * full_attn_gain).astype(BF16)
    query_raw = matmul(normed_one, full_query)
    latent_all = matmul(normed_one, full_latent)
    latent_part = latent_all[:, :RANK]
    rope_key = latent_all[:, RANK:]
    scale_latent = inverse_rms(latent_part)
    latent_norm = latent_part * scale_latent
    latent_in = (latent_norm * full_latent_gain).astype(BF16)
    kv_raw = jnp.concatenate([matmul(latent_in, up_left), matmul(latent_in, up_right)], axis=1)
    allowed, cosine_table, sine_table = tables(doc_ids[0])
    queries, key_rows, value_rows = prepare(query_raw, kv_raw, rope_key, cosine_table, sine_table)
    head_out, weights = attend(queries, key_rows, value_rows, allowed)
    mixed = hidden_wide + product("tv,dv->td", head_out, full_output)
    scale_two = inverse_rms(mixed)
    norm_two = mixed * scale_two
    normed_two = (norm_two * full_ffn_gain).astype(BF16)

    rows_in = [exchange(matmul(selector[u], normed_two).astype(BF16)) for u in range(local_units)]

    shared_width = shared_in.shape[1]
    full_shared_in = gathered_shared[:, :shared_width]
    full_shared_out = gathered_shared[:, shared_width:]
    shared_pre = matmul(normed_two, full_shared_in)
    shared_act = swiglu_forward(shared_pre)
    grad_shared_act = matmul(out_grad, full_shared_out)
    grad_shared_pre = swiglu_backward(shared_pre, grad_shared_act)
    grad_shared = jnp.concatenate(
        [
            product("td,tf->df", normed_two, grad_shared_pre).astype(BF16),
            product("td,tf->df", out_grad, shared_act).astype(BF16),
        ],
        axis=1,
    )
    owned_shared = lax.psum_scatter(grad_shared, "fsdp", scatter_dimension=0, tiled=True)
    shared_y = product("tf,df->td", shared_act, full_shared_out)
    shared_dx = product("tf,df->td", grad_shared_pre, full_shared_in)

    back_dx, back_out, grads_in, grads_out = [], [], [], []
    for u in range(local_units):
        weight_in = expert_in[u * pieces : (u + 1) * pieces]
        weight_out = expert_out[u * pieces : (u + 1) * pieces]
        pre_act = product("rd,pdf->prf", rows_in[u], weight_in)
        activation = swiglu_forward(pre_act)
        grad_act = product("rd,pfd->prf", grad_rows[u], weight_out)
        grad_pre = swiglu_backward(pre_act, grad_act)
        back_dx.append(exchange(product("prf,pdf->rd", grad_pre, weight_in).astype(BF16)))
        back_out.append(exchange(product("prf,pfd->rd", activation, weight_out).astype(BF16)))
        grads_out.append(product("prf,rd->pfd", activation, grad_rows[u]))
        grads_in.append(product("rd,prf->pdf", rows_in[u], grad_pre))
    grad_expert_in = jnp.concatenate(grads_in, axis=0)
    grad_expert_out = jnp.concatenate(grads_out, axis=0)

    routed_dx = sum(product("rt,rd->td", selector[u], back_dx[u]) for u in range(local_units))
    gate_high = lax.reduce_precision(gate_wide, 8, 7)
    gate_low = (gate_wide - gate_high).astype(BF16)
    gate_high = gate_high.astype(BF16)
    routed_y = sum(
        product("rt,rd->td", gate_high[u], back_out[u])
        + product("rt,rd->td", gate_low[u], back_out[u])
        for u in range(local_units)
    )
    layer_out = (mixed + shared_y + routed_y).astype(BF16)

    grad_normed_two = shared_dx + routed_dx
    grad_ffn_gain = jnp.sum(grad_normed_two * norm_two, axis=0)
    grad_norm_two = grad_normed_two * full_ffn_gain
    grad_mixed = out_grad.astype(F32) + scale_two * (
        grad_norm_two - norm_two * jnp.mean(grad_norm_two * norm_two, axis=-1, keepdims=True)
    )
    mixed_low = grad_mixed.astype(BF16)
    grad_output_proj = product("td,tv->dv", mixed_low, head_out)
    grad_heads = matmul(mixed_low, full_output).astype(BF16)
    grad_query_wide, grad_kv_wide, grad_rope = attend_back(
        queries, key_rows, value_rows, weights, cosine_table, sine_table, head_out, grad_heads
    )
    grad_query_raw = grad_query_wide.astype(BF16)
    grad_kv = grad_kv_wide.astype(BF16)
    kv_left, kv_right = grad_kv[:, :UW], grad_kv[:, UW:]
    grad_up = jnp.stack(
        [
            product("tr,tk->rk", latent_in, kv_left).astype(BF16).reshape(devices, half, UW),
            product("tr,tk->rk", latent_in, kv_right).astype(BF16).reshape(devices, half, UW),
        ],
        axis=1,
    ).reshape(D, UW)
    grad_latent_in = product("tk,rk->tr", kv_left, up_left) + product("tk,rk->tr", kv_right, up_right)
    grad_latent_gain = jnp.sum(grad_latent_in * latent_norm, axis=0)
    grad_norm_latent = grad_latent_in * full_latent_gain
    grad_latent = scale_latent * (
        grad_norm_latent
        - latent_norm * jnp.mean(grad_norm_latent * latent_norm, axis=-1, keepdims=True)
    )
    grad_latent_all = jnp.concatenate([grad_latent, grad_rope], axis=-1).astype(BF16)
    grad_query_proj = product("td,tq->dq", normed_one, grad_query_raw)
    grad_latent_proj = product("td,tq->dq", normed_one, grad_latent_all)
    grad_normed_one = product("tq,dq->td", grad_query_raw, full_query) + product(
        "tq,dq->td", grad_latent_all, full_latent
    )
    grad_attn_gain = jnp.sum(grad_normed_one * norm_one, axis=0)
    grad_norm_one = grad_normed_one * full_attn_gain
    input_grad = grad_mixed + scale_one * (
        grad_norm_one - norm_one * jnp.mean(grad_norm_one * norm_one, axis=-1, keepdims=True)
    )
    latent_gain_column = jnp.concatenate(
        [grad_latent_gain.reshape(devices, half), jnp.zeros((devices, own - half), F32)], axis=1
    ).reshape(D)
    grad_gains = jnp.concatenate(
        [
            jnp.stack([grad_attn_gain, grad_ffn_gain, latent_gain_column], axis=1),
            jnp.zeros((D, ATT_W - gain_at - 3), F32),
        ],
        axis=1,
    ).astype(BF16)
    grad_packed = jnp.concatenate(
        [
            grad_query_proj.astype(BF16),
            grad_output_proj.astype(BF16),
            grad_up,
            grad_latent_proj.astype(BF16),
            grad_gains,
        ],
        axis=1,
    )
    owned = lax.psum_scatter(grad_packed, "fsdp", scatter_dimension=0, tiled=True).astype(F32)
    owned_shared = owned_shared.astype(F32)
    owned_up = owned[:, QW + OW : QW + OW + UW]
    return (
        layer_out,
        input_grad,
        owned[:, gain_at],
        owned[:, :QW],
        owned[:, QW + OW + UW : gain_at],
        owned[:half, gain_at + 2],
        jnp.concatenate([owned_up[:half], owned_up[half:]], axis=1),
        owned[:, QW : QW + OW],
        owned[:, gain_at + 1],
        owned_shared[:, :shared_width],
        owned_shared[:, shared_width:],
        grad_expert_in,
        grad_expert_out,
    )


def solution(mesh):
    rows = P("fsdp", None)
    flat = P("fsdp")
    cube = P("fsdp", None, None)
    in_specs = (rows,) * 5 + (flat, rows, rows, flat, rows, rows, flat, rows, rows, cube, cube)
    out_specs = (rows, rows, flat, rows, rows, flat, rows, rows, flat, rows, rows, cube, cube)
    return jax.shard_map(body, mesh=mesh, in_specs=in_specs, out_specs=out_specs, check_vma=False)
```

time: 1400 us -> 568 us (0.41)
  waiting for transfers between devices: 934 us -> 241 us
  blocking collectives: 167 us -> 0 us
  other arithmetic: 19.2 us -> 57.8 us
  local copies, waits for them, and re-layouts: 93.3 us -> 69.9 us
    reduce_scatter x5 -> x2, waiting for transfers between devices: 512 us -> 30.4 us  [the longest x1 30.4 us: body(): lax.psum_scatter(grad_packed, 'fsdp', scatter_dimension=0, tiled=True)]
    unnamed x2 -> x0, blocking collectives: 167 us -> none
    all_gather x6 -> x2, waiting for transfers between devices: 246 us -> 134 us  [the longest x1 73 us: body(): gathered = lax.all_gather(packed, 'fsdp', axis=0, tiled=True)]
    all_to_all x4 -> x8, waiting for transfers between devices: 172 us -> 76.8 us  [exchange(): lax.all_to_all(rows.reshape(devices, CAP, D), 'fsdp', split_axis=0, conca...]
    concatenate x0 -> x6, other arithmetic: none -> 34.2 us  [the longest x1 17 us: body(): grad_expert_in = jnp.concatenate(grads_in, axis=0)]
    gather x2 -> x0, local copies, waits for them, and re-layouts: 21.1 us -> none  [the longest x1 10.6 us: body(): back_dx.reshape(total_rows, D)[send_row].astype(jnp.float32)]
    all_to_all x4 -> x0, local copies, waits for them, and re-layouts: 20.2 us -> none  [the longest x1 5.07 us: body(): lax.all_to_all(send_in, 'fsdp', split_axis=1, concat_axis=1, tiled=True)]
    unnamed x78 -> x139, local copies, waits for them, and re-layouts: 11.2 us -> 30.2 us
  transfers between devices with their start and end apart: 16 -> 12, of which waited for: 10 -> 8; matrix products, arithmetic and copies ran while one was open for 14% -> 44% of each run, Pallas kernels for 0% -> 0%
where the time goes in v1:
time: 568 us; the launch traced here: 557 us
  waiting for transfers between devices  241 us (42%)
  matrix products  138 us (24%)
  local copies, waits for them, and re-layouts  69.9 us (12%)
  other arithmetic  57.8 us (10%)
  starting transfers between devices  35 us (6%)
  between operations  15.3 us (3%)
    dot_general x38, matrix products, product(): jnp.einsum(pattern, left_side, right_side, preferred_element_type=F32)  116 us
    all_to_all x8, waiting for transfers between devices, exchange(): lax.all_to_all(rows.reshape(devices, CAP, D), 'fsdp', split_axis=0, conca...  76.8 us
    all_gather x1, waiting for transfers between devices, body(): gathered = lax.all_gather(packed, 'fsdp', axis=0, tiled=True)  73 us
    all_gather x1, waiting for transfers between devices, body(): lax.all_gather(jnp.concatenate([shared_in, shared_out], axis=1), 'fsdp',...  60.6 us
    all_to_all x8, starting transfers between devices, exchange(): lax.all_to_all(rows.reshape(devices, CAP, D), 'fsdp', split_axis=0, conca...  34.1 us
    reduce_scatter x1, waiting for transfers between devices, body(): lax.psum_scatter(grad_packed, 'fsdp', scatter_dimension=0, tiled=True)  30.4 us
    unnamed x139, local copies, waits for them, and re-layouts  30.2 us
    dot_general x12, matrix products, matmul(): return jnp.dot(left_side, right_side, preferred_element_type=F32)  22.7 us
  transfers between devices with their start and end apart: 12, of which 8 were waited for; matrix products, arithmetic and copies ran while one was open for 44% of the time, Pallas kernels for 0%

profile of v1, /device:TPU:0, one launch (start us, length us, event | category | flops | bytes accessed | tf_op | source)
XLA Modules:
  0.0 557.4 jit_solution(1770833153453059210)
XLA Ops:
  16.3 2.4 multiply_convert_fusion.2
  18.7 7.5 %all-to-all-start.6 = ((bf16[32,16,1024]{2,1,0:T(8,128)(2,1)}), bf16[32,16,1024]{2,1,0:T(8,128)(2,1)}, u32[]{:S(2)}, u32[]{:S(2)}) async-start(bf16[32,16,1024]{2,1,0:T(8,128)(2,1)} %bitcast.46), calls=%async_computation.6 | async-start | bytes 2097152 | tf_op jit(solution)/shard_map/all_to_all | solution.py:212
  29.4 73.0 %all-gather.3.cloned.1.call-done = bf16[1024,4224]{1,0:T(8,128)(2,1)} async-done(((bf16[32,4224]{1,0:T(8,128)(2,1)}), bf16[1024,4224]{1,0:T(8,128)(2,1)}) %all-gather.3.cloned.1.call-update) | async-done | bytes 8650768 | tf_op jit(solution)/shard_map/all_gather | solution.py:184
  107.9 3.4 fusion.30
  114.0 3.4 all-to-all-start.4
  124.2 2.3 convolution_convert_fusion.10
  126.5 2.6 multiply_reduce_fusion.3
  131.3 60.6 %all-gather.5.cloned.1.call-done = bf16[1024,4224]{1,0:T(8,128)(2,1)} async-done(((bf16[32,4224]{1,0:T(8,128)(2,1)}), bf16[1024,4224]{1,0:T(8,128)(2,1)}) %all-gather.5.cloned.1.call-update) | async-done | bytes 8650768 | tf_op jit(solution)/shard_map/all_gather | solution.py:185
  191.8 4.7 fusion.3
  196.5 3.4 all-to-all-start
  200.4 2.9 multiply_convert_fusion.5
  206.1 3.6 pad_maximum_fusion.2
  212.0 14.1 %all-to-all-done = bf16[32,16,1024]{2,1,0:T(8,128)(2,1)} async-done(((bf16[32,16,1024]{2,1,0:T(8,128)(2,1)}), bf16[32,16,1024]{2,1,0:T(8,128)(2,1)}, u32[]{:S(2)}, u32[]{:S(2)}) %all-to-all-start) | async-done | bytes 1048608 | tf_op jit(solution)/shard_map/all_to_all | solution.py:212
  226.1 3.7 all-to-all-start.2
  229.8 6.5 %fusion.13 = f32[2,512,1408]{2,1,0:T(8,128)S(1)} fusion(bf16[512,1024,1]{1,0,2:T(8,128)(2,1)} %bitcast.22, bf16[4,1024,1408]{2,1,0:T(8,128)(2,1)} %param.30), kind=kOutput, calls=%fused_computation.19 | convolution fusion | flops 2952790016 | bytes 12582912 | tf_op jit(solution)/shard_map/rd,pdf->prf/dot_general | solution.py:33
  236.4 6.3 %fusion.24 = (bf16[2,512,704]{2,1,0:T(8,128)(2,1)S(1)}, bf16[2,512,704]{2,1,0:T(8,128)(2,1)S(1)}, bf16[2,512,704]{2,1,0:T(8,128)(2,1)}) fusion(f32[2,512,1408]{2,1,0:T(8,128)S(1)} %fusion.13, bf16[512,1024,1]{1,0,2:T(8,128)(2,1)} %bitcast.41, bf16[4,704,1024]{2,1,0:T(8,128)(2,1)} %param.31), kind=kOutput, calls=%fused_computation.32 | convolution fusion | flops 1487208448 | bytes 14024704 | tf_op jit(solution)/shard_map/rd,pfd->prf/dot_general | solution.py:33
  244.4 4.1 bitcast_convert_fusion.1
  248.6 7.4 %all-to-all-done.2 = bf16[32,16,1024]{2,1,0:T(8,128)(2,1)} async-done(((bf16[32,16,1024]{2,1,0:T(8,128)(2,1)}), bf16[32,16,1024]{2,1,0:T(8,128)(2,1)}, u32[]{:S(2)}, u32[]{:S(2)}) %all-to-all-start.2) | async-done | bytes 1048608 | tf_op jit(solution)/shard_map/all_to_all | solution.py:212
  256.0 3.9 all-to-all-start.5
  260.0 6.5 %fusion.16 = f32[2,512,1408]{2,1,0:T(8,128)S(1)} fusion(bf16[512,1024,1]{1,0,2:T(8,128)(2,1)} %bitcast.32, bf16[4,1024,1408]{2,1,0:T(8,128)(2,1)} %param.30), kind=kOutput, calls=%fused_computation.20 | convolution fusion | flops 2952790016 | bytes 12582912 | tf_op jit(solution)/shard_map/rd,pdf->prf/dot_general | solution.py:33
  266.4 6.1 %fusion.21 = (bf16[2,512,704]{2,1,0:T(8,128)(2,1)S(1)}, bf16[2,512,704]{2,1,0:T(8,128)(2,1)S(1)}, bf16[2,512,704]{2,1,0:T(8,128)(2,1)}) fusion(f32[2,512,1408]{2,1,0:T(8,128)S(1)} %fusion.16, bf16[512,1024,1]{1,0,2:T(8,128)(2,1)} %bitcast.48, bf16[4,704,1024]{2,1,0:T(8,128)(2,1)} %param.31), kind=kOutput, calls=%fused_computation.27 | convolution fusion | flops 1487208448 | bytes 14024704 | tf_op jit(solution)/shard_map/rd,pfd->prf/dot_general | solution.py:33
  274.3 4.1 bitcast_convert_fusion
  278.4 29.2 %all-to-all-done.5 = bf16[32,16,1024]{2,1,0:T(8,128)(2,1)} async-done(((bf16[32,16,1024]{2,1,0:T(8,128)(2,1)}), bf16[32,16,1024]{2,1,0:T(8,128)(2,1)}, u32[]{:S(2)}, u32[]{:S(2)}) %all-to-all-start.5) | async-done | bytes 1048608 | tf_op jit(solution)/shard_map/all_to_all | solution.py:212
  307.6 4.6 all-to-all-start.7
  312.6 2.2 fusion.73
  314.7 5.5 fusion.1
  321.9 21.7 %all-to-all-done.7 = bf16[32,16,1024]{2,1,0:T(8,128)(2,1)} async-done(((bf16[32,16,1024]{2,1,0:T(8,128)(2,1)}), bf16[32,16,1024]{2,1,0:T(8,128)(2,1)}, u32[]{:S(2)}, u32[]{:S(2)}) %all-to-all-start.7) | async-done | bytes 1048608 | tf_op jit(solution)/shard_map/all_to_all | solution.py:212
  343.5 2.5 multiply_reduce_fusion
  347.2 2.3 fusion.83
  357.8 2.3 fusion.86
  370.3 3.9 fusion.103
  379.8 2.1 convolution_convert_fusion.3
  383.7 13.5 %concatenate.86 = bf16[1024,4224]{1,0:T(8,128)(2,1)} concatenate(bf16[1024,1536]{1,0:T(8,128)(2,1)S(1)} %convolution_convert_fusion.1, bf16[1024,1024]{1,0:T(8,128)(2,1)} %convolution_convert_fusion.3, bf16[1024,1024]{1,0:T(8,128)(2,1)} %bitcast.189, bf16[1024,576]{1,0:T(8,128)(2,1)} %copy.165, bf16[1024,1]{1,0:T(8,128)(2,1)} %stack.14, bf16[1024,1]{1,0:T(8,128)(2,1)} %stack.15, ...), dimensions={1} | concatenate | bytes 17301504 | tf_op jit(solution)/shard_map/concatenate | solution.py:350
  397.3 5.2 bitcast_convert_fusion.2
  402.5 4.0 all-to-all-start.3
  407.6 4.9 bitcast_convert_fusion.3
  412.4 8.0 %convolution_bitcast_fusion = f32[2,1024,1408]{1,2,0:T(8,128)} fusion(bf16[512,1024,1]{1,0,2:T(8,128)(2,1)} %bitcast.32, bf16[2,512,704]{2,1,0:T(8,128)(2,1)S(1)} %copy-done.62, bf16[2,512,704]{2,1,0:T(8,128)(2,1)S(1)} %copy-done.60), kind=kOutput, calls=%fused_computation.4 | convolution fusion | flops 2958557184 | bytes 15466496 | tf_op jit(solution)/shard_map/rd,prf->pdf/dot_general | solution.py:33
  420.4 7.8 %convolution_bitcast_fusion.1 = f32[2,1024,1408]{1,2,0:T(8,128)} fusion(bf16[512,1024,1]{1,0,2:T(8,128)(2,1)} %bitcast.22, bf16[2,512,704]{2,1,0:T(8,128)(2,1)S(1)} %copy-done.58, bf16[2,512,704]{2,1,0:T(8,128)(2,1)S(1)} %copy-done.56), kind=kOutput, calls=%fused_computation.5 | convolution fusion | flops 2958557184 | bytes 15466496 | tf_op jit(solution)/shard_map/rd,prf->pdf/dot_general | solution.py:33
  428.2 4.4 all-to-all-done.3
  432.7 3.6 all-to-all-start.1
  436.3 17.0 %pad_maximum_fusion = f32[4,1024,1408]{1,2,0:T(8,128)} fusion(f32[2,1024,1408]{1,2,0:T(8,128)} %convolution_bitcast_fusion, f32[2,1024,1408]{1,2,0:T(8,128)} %convolution_bitcast_fusion.1), kind=kLoop, calls=%fused_computation.1 | loop fusion | flops 5767168 | bytes 46137344 | tf_op jit(solution)/shard_map/concatenate | solution.py:286
  453.3 23.4 %copy.174 = f32[4,1024,1408]{2,1,0:T(8,128)} copy(f32[4,1024,1408]{1,2,0:T(8,128)} %pad_maximum_fusion) | data formatting | bytes 46137344
  476.6 6.1 %fusion.165 = f32[2,704,1024]{2,1,0:T(8,128)} fusion(bf16[2,512,704]{2,1,0:T(8,128)(2,1)} %get-tuple-element.79, bf16[512,1024,1]{1,0,2:T(8,128)(2,1)} %bitcast.48), kind=kOutput, calls=%fused_computation.247 | convolution fusion | flops 1476395008 | bytes 8257536 | tf_op jit(solution)/shard_map/prf,rd->pfd/dot_general | solution.py:33
  482.7 5.4 fusion.164
  488.1 11.2 %pad_maximum_fusion.1 = f32[4,704,1024]{2,1,0:T(8,128)} fusion(f32[2,704,1024]{2,1,0:T(8,128)} %fusion.165, f32[2,704,1024]{2,1,0:T(8,128)} %fusion.164), kind=kLoop, calls=%fused_computation.2 | loop fusion | flops 2883584 | bytes 23068672 | tf_op jit(solution)/shard_map/concatenate | solution.py:287
  502.0 2.1 fusion.102
  504.8 3.6 fusion.80
  511.7 30.4 %reduce-scatter.3.cloned.1.call-done = bf16[32,4224]{1,0:T(8,128)(2,1)} async-done(((bf16[1024,4224]{1,0:T(8,128)(2,1)}), bf16[32,4224]{1,0:T(8,128)(2,1)}) %reduce-scatter.3.cloned.1.call-update) | async-done | bytes 270352 | tf_op jit(solution)/shard_map/reduce_scatter | solution.py:360
  (259 shorter events, 82.6 us)
Async XLA Ops:
  7.2 19.1 %copy-start.54 = (s32[1,128]{1,0:T(1,128)S(1)}, s32[1,128]{1,0:T(1,128)}, u32[]{:S(2)}) copy-start(s32[1,128]{1,0:T(1,128)} %param.18) | copy-start | bytes 1540
  7.2 19.2 %copy-start.4 = (bf16[128,1024]{1,0:T(8,128)(2,1)S(1)}, bf16[128,1024]{1,0:T(8,128)(2,1)}, u32[]{:S(2)}) copy-start(bf16[128,1024]{1,0:T(8,128)(2,1)} %param.16) | copy-start | bytes 786436
  7.2 95.2 %all-gather.3.cloned.1.call-start = ((), (), s32[]{:S(2)}) async-start(), calls=%async_computation.10 | async-start | bytes 8921088 | tf_op jit(solution)/shard_map/all_gather | solution.py:184
  10.3 17.6 %copy-start.5 = (bf16[128,1024]{1,0:T(8,128)(2,1)S(1)}, bf16[128,1024]{1,0:T(8,128)(2,1)}, u32[]{:S(2)}) copy-start(bf16[128,1024]{1,0:T(8,128)(2,1)} %param.17) | copy-start | bytes 786436
  12.1 179.7 %all-gather.5.cloned.1.call-start = ((), (), s32[]{:S(2)}) async-start(), calls=%async_computation.11 | async-start | bytes 8921088 | tf_op jit(solution)/shard_map/all_gather | solution.py:185
  16.3 87.5 %copy-start.20 = (pred[1,32,16,128]{3,2,1,0:T(8,128)(4,1)}, pred[1,32,16,128]{3,2,1,0:T(8,128)(4,1)S(1)}, u32[]{:S(2)}) copy-start(pred[1,32,16,128]{3,2,1,0:T(8,128)(4,1)S(1)} %get-tuple-element.94) | copy-start | bytes 196612
  16.3 87.5 %copy-start.23 = (pred[1,32,16,128]{3,2,1,0:T(8,128)(4,1)}, pred[1,32,16,128]{3,2,1,0:T(8,128)(4,1)S(1)}, u32[]{:S(2)}) copy-start(pred[1,32,16,128]{3,2,1,0:T(8,128)(4,1)S(1)} %get-tuple-element.95) | copy-start | bytes 196612
  18.7 95.3 %all-to-all-start.6 = ((bf16[32,16,1024]{2,1,0:T(8,128)(2,1)}), bf16[32,16,1024]{2,1,0:T(8,128)(2,1)}, u32[]{:S(2)}, u32[]{:S(2)}) async-start(bf16[32,16,1024]{2,1,0:T(8,128)(2,1)} %bitcast.46), calls=%async_computation.6 | async-start | bytes 2097152 | tf_op jit(solution)/shard_map/all_to_all | solution.py:212
  26.2 91.2 %copy-start.49 = (f32[32]{0:T(128)}, f32[32]{0:T(128)S(1)}, u32[]{:S(2)}) copy-start(f32[32]{0:T(128)S(1)} %multiply_exponential_fusion) | copy-start | bytes 388
  26.5 81.4 %copy-start.45 = (f32[128]{0:T(128)}, f32[128]{0:T(128)S(1)}, u32[]{:S(2)}) copy-start(f32[128]{0:T(128)S(1)} %add_rsqrt_fusion.2) | copy-start | bytes 1540
  26.5 90.9 %copy-start.50 = (f32[128]{0:T(128)}, f32[128]{0:T(128)S(1)}, u32[]{:S(2)}) copy-start(f32[128]{0:T(128)S(1)} %subtract_convert_fusion.2) | copy-start | bytes 1540
  103.8 8.4 %copy-start.42 = (f32[512]{0:T(512)}, f32[512]{0:T(512)S(1)}, u32[]{:S(2)}) copy-start(f32[512]{0:T(512)S(1)} %reshape.348) | copy-start | bytes 6148
  105.8 5.5 copy-start.35
  107.8 9.6 %copy-start.6 = (f32[128,576]{0,1:T(8,128)}, f32[128,576]{0,1:T(8,128)S(1)}, u32[]{:S(2)}) copy-start(f32[128,576]{0,1:T(8,128)S(1)} %fusion.89) | copy-start | bytes 884740
  114.0 82.5 %all-to-all-start.4 = ((bf16[32,16,1024]{2,1,0:T(8,128)(2,1)}), bf16[32,16,1024]{2,1,0:T(8,128)(2,1)}, u32[]{:S(2)}, u32[]{:S(2)}) async-start(bf16[32,16,1024]{2,1,0:T(8,128)(2,1)} %bitcast.39), calls=%async_computation.4 | async-start | bytes 2097152 | tf_op jit(solution)/shard_map/all_to_all | solution.py:212
  119.3 9.9 %copy-start.16 = (bf16[128,8,128]{0,2,1:T(8,128)(2,1)}, bf16[128,8,128]{0,2,1:T(8,128)(2,1)S(1)}, u32[]{:S(2)}) copy-start(bf16[128,8,128]{0,2,1:T(8,128)(2,1)S(1)} %slice.467) | copy-start | bytes 786436
  120.7 5.8 %copy-start.8 = (bf16[128,2048]{0,1:T(8,128)(2,1)}, bf16[128,2048]{0,1:T(8,128)(2,1)S(1)}, u32[]{:S(2)}) copy-start(bf16[128,2048]{0,1:T(8,128)(2,1)S(1)} %copy.196) | copy-start | bytes 1572868
  129.1 216.9 %copy-start = (f32[128,1024]{1,0:T(8,128)}, f32[128,1024]{1,0:T(8,128)S(1)}, u32[]{:S(2)}) copy-start(f32[128,1024]{1,0:T(8,128)S(1)} %get-tuple-element.108) | copy-start | bytes 1572868
  196.5 29.6 %all-to-all-start = ((bf16[32,16,1024]{2,1,0:T(8,128)(2,1)}), bf16[32,16,1024]{2,1,0:T(8,128)(2,1)}, u32[]{:S(2)}, u32[]{:S(2)}) async-start(bf16[32,16,1024]{2,1,0:T(8,128)(2,1)} %bitcast.195), calls=%async_computation | async-start | bytes 2097152 | tf_op jit(solution)/shard_map/all_to_all | solution.py:212
  199.9 308.5 %reduce-scatter.5.cloned.1.call-start = ((), (), s32[]{:S(2)}) async-start(), calls=%async_computation.13 | async-start | bytes 8921088 | tf_op jit(solution)/shard_map/reduce_scatter | solution.py:270
  226.1 29.9 %all-to-all-start.2 = ((bf16[32,16,1024]{2,1,0:T(8,128)(2,1)}), bf16[32,16,1024]{2,1,0:T(8,128)(2,1)}, u32[]{:S(2)}, u32[]{:S(2)}) async-start(bf16[32,16,1024]{2,1,0:T(8,128)(2,1)} %bitcast.196), calls=%async_computation.2 | async-start | bytes 2097152 | tf_op jit(solution)/shard_map/all_to_all | solution.py:212
  229.8 14.6 %slice-start.1 = ((s8[11534336]{0:T(1024)(128)(4,1)}), s8[4194304]{0:T(1024)(128)(4,1)S(1)}, s32[]{:S(2)}) async-start(s8[11534336]{0:T(1024)(128)(4,1)} %bitcast.226), calls=%async_computation.15 | async-start | bytes 8388608
  229.8 14.6 %slice-start.2 = ((s8[11534336]{0:T(1024)(128)(4,1)}), s8[4194304]{0:T(1024)(128)(4,1)S(1)}, s32[]{:S(2)}) async-start(s8[11534336]{0:T(1024)(128)(4,1)} %bitcast.226), calls=%async_computation.16 | async-start | bytes 8388608
  236.4 8.0 %slice-start.3 = ((s8[11534336]{0:T(1024)(128)(4,1)}), s8[3145728]{0:T(1024)(128)(4,1)S(1)}, s32[]{:S(2)}) async-start(s8[11534336]{0:T(1024)(128)(4,1)} %bitcast.226), calls=%async_computation.17 | async-start | bytes 6291456
  256.0 51.6 %all-to-all-start.5 = ((bf16[32,16,1024]{2,1,0:T(8,128)(2,1)}), bf16[32,16,1024]{2,1,0:T(8,128)(2,1)}, u32[]{:S(2)}, u32[]{:S(2)}) async-start(bf16[32,16,1024]{2,1,0:T(8,128)(2,1)} %bitcast.208), calls=%async_computation.5 | async-start | bytes 2097152 | tf_op jit(solution)/shard_map/all_to_all | solution.py:212
  259.9 14.3 %slice-start.4 = ((s8[11534336]{0:T(1024)(128)(4,1)}), s8[4194304]{0:T(1024)(128)(4,1)S(1)}, s32[]{:S(2)}) async-start(s8[11534336]{0:T(1024)(128)(4,1)} %bitcast.228), calls=%async_computation.18 | async-start | bytes 8388608
  259.9 14.3 %slice-start.5 = ((s8[11534336]{0:T(1024)(128)(4,1)}), s8[4194304]{0:T(1024)(128)(4,1)S(1)}, s32[]{:S(2)}) async-start(s8[11534336]{0:T(1024)(128)(4,1)} %bitcast.228), calls=%async_computation.19 | async-start | bytes 8388608
  266.4 7.9 %slice-start.6 = ((s8[11534336]{0:T(1024)(128)(4,1)}), s8[3145728]{0:T(1024)(128)(4,1)S(1)}, s32[]{:S(2)}) async-start(s8[11534336]{0:T(1024)(128)(4,1)} %bitcast.228), calls=%async_computation.20 | async-start | bytes 6291456
  274.3 38.3 %copy-start.43 = (pred[128,128]{0,1:T(8,128)(4,1)S(1)}, pred[128,128]{0,1:T(8,128)(4,1)}, u32[]{:S(2)}) copy-start(pred[128,128]{0,1:T(8,128)(4,1)} %compare_and_fusion) | copy-start | bytes 49156
  278.4 36.3 %copy-start.29 = (bf16[128,1408]{1,0:T(8,128)(2,1)S(1)}, bf16[128,1408]{1,0:T(8,128)(2,1)}, u32[]{:S(2)}) copy-start(bf16[128,1408]{1,0:T(8,128)(2,1)} %copy-done.28) | copy-start | bytes 1081348
  307.6 35.9 %all-to-all-start.7 = ((bf16[32,16,1024]{2,1,0:T(8,128)(2,1)}), bf16[32,16,1024]{2,1,0:T(8,128)(2,1)}, u32[]{:S(2)}, u32[]{:S(2)}) async-start(bf16[32,16,1024]{2,1,0:T(8,128)(2,1)} %bitcast.207), calls=%async_computation.7 | async-start | bytes 2097152 | tf_op jit(solution)/shard_map/all_to_all | solution.py:212
  312.3 229.8 %reduce-scatter.3.cloned.1.call-start = ((), (), s32[]{:S(2)}) async-start(), calls=%async_computation.12 | async-start | bytes 8921088 | tf_op jit(solution)/shard_map/reduce_scatter | solution.py:360
  314.7 5.5 copy-start.22
  347.2 32.6 %copy-start.2 = (f32[128,1024]{1,0:T(8,128)}, f32[128,1024]{1,0:T(8,128)S(1)}, u32[]{:S(2)}) copy-start(f32[128,1024]{1,0:T(8,128)S(1)} %multiply_add_fusion) | copy-start | bytes 1572868
  360.1 5.1 copy-start.36
  360.1 5.1 copy-start.46
  361.6 5.6 copy-start.39
  361.6 6.6 %copy-start.15 = (bf16[128,8,128]{0,2,1:T(8,128)(2,1)S(1)}, bf16[128,8,128]{0,2,1:T(8,128)(2,1)}, u32[]{:S(2)}) copy-start(bf16[128,8,128]{0,2,1:T(8,128)(2,1)} %slice.466) | copy-start | bytes 786436
  368.2 6.0 %copy-start.11 = (bf16[128,8,192]{0,2,1:T(8,128)(2,1)}, bf16[128,8,192]{0,2,1:T(8,128)(2,1)S(1)}, u32[]{:S(2)}) copy-start(bf16[128,8,192]{0,2,1:T(8,128)(2,1)S(1)} %pad_maximum_fusion.20) | copy-start | bytes 1179652
  397.3 9.3 %copy-start.26 = (s32[2,32,128]{2,1,0:T(8,128)S(1)}, s32[2,32,128]{2,1,0:T(8,128)}, u32[]{:S(2)}) copy-start(s32[2,32,128]{2,1,0:T(8,128)} %copy-done.25) | copy-start | bytes 98308
  397.3 9.3 %copy-start.33 = (f32[2,32,128]{2,1,0:T(8,128)S(1)}, f32[2,32,128]{2,1,0:T(8,128)}, u32[]{:S(2)}) copy-start(f32[2,32,128]{2,1,0:T(8,128)} %copy-done.32) | copy-start | bytes 98308
  397.3 10.3 %copy-start.9 = (bf16[2,512,704]{2,1,0:T(8,128)(2,1)S(1)}, bf16[2,512,704]{2,1,0:T(8,128)(2,1)}, u32[]{:S(2)}) copy-start(bf16[2,512,704]{2,1,0:T(8,128)(2,1)} %get-tuple-element.80) | copy-start | bytes 4325380
  402.5 30.2 %all-to-all-start.3 = ((bf16[32,16,1024]{2,1,0:T(8,128)(2,1)}), bf16[32,16,1024]{2,1,0:T(8,128)(2,1)S(1)}, u32[]{:S(2)}, u32[]{:S(2)}) async-start(bf16[32,16,1024]{2,1,0:T(8,128)(2,1)} %bitcast.206), calls=%async_computation.3 | async-start | bytes 2097152 | tf_op jit(solution)/shard_map/all_to_all | solution.py:212
  407.6 4.9 copy-start.62
  412.4 8.0 %copy-start.56 = (bf16[2,512,704]{2,1,0:T(8,128)(2,1)S(1)}, bf16[2,512,704]{2,1,0:T(8,128)(2,1)}, u32[]{:S(2)}) copy-start(bf16[2,512,704]{2,1,0:T(8,128)(2,1)} %copy-done.55) | copy-start | bytes 4325380
  412.4 8.0 %copy-start.58 = (bf16[2,512,704]{2,1,0:T(8,128)(2,1)S(1)}, bf16[2,512,704]{2,1,0:T(8,128)(2,1)}, u32[]{:S(2)}) copy-start(bf16[2,512,704]{2,1,0:T(8,128)(2,1)} %copy-done.57) | copy-start | bytes 4325380
  432.7 68.0 %all-to-all-start.1 = ((bf16[32,16,1024]{2,1,0:T(8,128)(2,1)}), bf16[32,16,1024]{2,1,0:T(8,128)(2,1)S(1)}, u32[]{:S(2)}, u32[]{:S(2)}) async-start(bf16[32,16,1024]{2,1,0:T(8,128)(2,1)} %bitcast.25), calls=%async_computation.1 | async-start | bytes 2097152 | tf_op jit(solution)/shard_map/all_to_all | solution.py:212
  476.6 6.1 %copy-start.10 = (bf16[2,512,704]{2,1,0:T(8,128)(2,1)S(1)}, bf16[2,512,704]{2,1,0:T(8,128)(2,1)}, u32[]{:S(2)}) copy-start(bf16[2,512,704]{2,1,0:T(8,128)(2,1)} %get-tuple-element.80) | copy-start | bytes 4325380
  (34 other events, 86.3 us)
Sparse Core Ops, SparseCore 0:
  12.3 90.1 all-gather.2
  105.3 86.4 all-gather.4
  209.9 162.3 reduce-scatter.4
  397.4 144.6 reduce-scatter.2

commit v2 on v1

v2 whole, which is shorter than its diff:
```python
import functools
import math

import jax
import jax.numpy as jnp
from jax import lax
from jax.experimental import pallas as pl
from jax.experimental.pallas import tpu as pltpu
from jax.sharding import PartitionSpec as P


D = 1024
H = 8
NOPE = 128
ROPE = 64
VDIM = 128
RANK = 512
EXPERTS = 64
CAP = 16
UW = H * (NOPE + VDIM) // 2
LW = RANK + ROPE

EPSILON = 1e-06
F32 = jnp.float32
BF16 = jnp.bfloat16


def matmul(left_side, right_side):
    return jnp.dot(left_side, right_side, preferred_element_type=F32)


def product(pattern, left_side, right_side):
    return jnp.einsum(pattern, left_side, right_side, preferred_element_type=F32)


def inverse_rms(values):
    return lax.rsqrt(jnp.mean(values * values, axis=-1, keepdims=True) + EPSILON)


def swiglu_parts(pre_act):
    middle = pre_act.shape[-1] // 2
    gate_pre = pre_act[..., :middle]
    up_pre = pre_act[..., middle:]
    return (gate_pre, up_pre, jax.nn.sigmoid(gate_pre))


def swiglu_forward(pre_act):
    gate_pre, up_pre, sigmoid_gate = swiglu_parts(pre_act)
    return (gate_pre * sigmoid_gate * up_pre).astype(BF16)


def swiglu_backward(pre_act, grad_act):
    gate_pre, up_pre, sigmoid_gate = swiglu_parts(pre_act)
    silu_value = gate_pre * sigmoid_gate
    slope = sigmoid_gate * (1.0 + gate_pre * (1.0 - sigmoid_gate))
    return jnp.concatenate([grad_act * up_pre * slope, grad_act * silu_value], axis=-1).astype(BF16)


def tables(documents):
    rows_here = documents.shape[0]
    indices = jnp.arange(rows_here, dtype=jnp.int32)
    same_doc = documents[:, None] == documents[None, :]
    starts = jnp.min(jnp.where(same_doc, indices[None, :], rows_here), axis=1)
    allowed = same_doc & (indices[None, :] <= indices[:, None])
    position = (indices - starts).astype(F32)
    frequency = jnp.exp(jnp.arange(ROPE // 2, dtype=F32) * (-2.0 * math.log(10000.0) / ROPE))
    angles = position[:, None] * frequency[None, :]
    return (allowed, jnp.cos(angles), jnp.sin(angles))


def nn(left_side, right_side):
    return lax.dot_general(
        left_side, right_side, (((1,), (0,)), ((), ())), preferred_element_type=F32
    )


def nt(left_side, right_side):
    return lax.dot_general(
        left_side, right_side, (((1,), (1,)), ((), ())), preferred_element_type=F32
    )


def tn(left_side, right_side):
    return lax.dot_general(
        left_side, right_side, (((0,), (0,)), ((), ())), preferred_element_type=F32
    )


def experts_kernel(rows, grads, w_in, w_out, dx, y, act, dpre, dx_sum, y_sum):
    piece = pl.program_id(1)
    middle = w_out.shape[1]
    pre_act = nn(rows[...], w_in[0])
    gate_pre = pre_act[:, :middle]
    up_pre = pre_act[:, middle:]
    sigmoid_gate = jax.nn.sigmoid(gate_pre)
    silu_value = gate_pre * sigmoid_gate
    act_low = (silu_value * up_pre).astype(BF16)
    act[0] = act_low
    grad_act = nt(grads[...], w_out[0])
    slope = sigmoid_gate * (1.0 + gate_pre * (1.0 - sigmoid_gate))
    dpre_low = jnp.concatenate([grad_act * up_pre * slope, grad_act * silu_value], axis=1).astype(BF16)
    dpre[0] = dpre_low
    dx_part = nt(dpre_low, w_in[0])
    y_part = nn(act_low, w_out[0])

    @pl.when(piece == 0)
    def _():
        dx_sum[...] = dx_part
        y_sum[...] = y_part

    @pl.when(piece > 0)
    def _():
        dx_sum[...] += dx_part
        y_sum[...] += y_part

    @pl.when(piece == pl.num_programs(1) - 1)
    def _():
        dx[...] = dx_sum[...].astype(BF16)
        y[...] = y_sum[...].astype(BF16)


def experts(rows, grads, w_in, w_out, unit, pieces):
    count, width = rows.shape
    first = unit * pieces
    double, middle = w_in.shape[2], w_out.shape[1]
    block = min(512, count)
    row_spec = pl.BlockSpec((block, width), lambda r, p: (r, 0))
    return pl.pallas_call(
        experts_kernel,
        grid=(count // block, pieces),
        in_specs=[
            row_spec,
            row_spec,
            pl.BlockSpec((1, width, double), lambda r, p: (first + p, 0, 0)),
            pl.BlockSpec((1, middle, width), lambda r, p: (first + p, 0, 0)),
        ],
        out_specs=[
            row_spec,
            row_spec,
            pl.BlockSpec((1, block, middle), lambda r, p: (p, r, 0)),
            pl.BlockSpec((1, block, double), lambda r, p: (p, r, 0)),
        ],
        out_shape=[
            jax.ShapeDtypeStruct((count, width), BF16),
            jax.ShapeDtypeStruct((count, width), BF16),
            jax.ShapeDtypeStruct((pieces, count, middle), BF16),
            jax.ShapeDtypeStruct((pieces, count, double), BF16),
        ],
        scratch_shapes=[pltpu.VMEM((block, width), F32), pltpu.VMEM((block, width), F32)],
        compiler_params=pltpu.CompilerParams(vmem_limit_bytes=60 * 2**20),
        cost_estimate=pl.CostEstimate(
            flops=2 * count * width * pieces * (2 * double + 2 * middle),
            bytes_accessed=pieces * (width + count) * (double + middle) * 2 + count * width * 8,
            transcendentals=count * middle * pieces,
        ),
        name="experts",
    )(rows, grads, w_in, w_out)


def expert_grads_kernel(rows, grads, act, dpre, *refs):
    grad_in, grad_out = refs[-2:]
    grad_in[0] = tn(rows[...], dpre[0])
    grad_out[0] = tn(act[0], grads[...])


def expert_grads(rows, grads, act, dpre, total, unit, late, held=None, chunk=256):
    count, width = rows.shape
    pieces, _, middle = act.shape
    first = unit * pieces
    double = dpre.shape[2]
    row_spec = pl.BlockSpec((count, chunk), lambda p, k: (0, k))
    operands = [rows, grads, act, dpre]
    in_specs = [
        row_spec,
        row_spec,
        pl.BlockSpec((1, count, middle), lambda p, k: (p, 0, 0)),
        pl.BlockSpec((1, count, double), lambda p, k: (p, 0, 0)),
    ]
    if late is not None:
        operands.append(late)
        in_specs.append(pl.BlockSpec(memory_space=pl.ANY))
    aliases = {}
    if held is not None:
        operands += list(held)
        in_specs += [pl.BlockSpec(memory_space=pl.ANY)] * 2
        aliases = {len(operands) - 2: 0, len(operands) - 1: 1}
    return pl.pallas_call(
        expert_grads_kernel,
        grid=(pieces, width // chunk),
        in_specs=in_specs,
        out_specs=[
            pl.BlockSpec((1, chunk, double), lambda p, k: (first + p, k, 0)),
            pl.BlockSpec((1, middle, chunk), lambda p, k: (first + p, 0, k)),
        ],
        out_shape=[
            jax.ShapeDtypeStruct((total, width, double), F32),
            jax.ShapeDtypeStruct((total, middle, width), F32),
        ],
        input_output_aliases=aliases,
        compiler_params=pltpu.CompilerParams(vmem_limit_bytes=60 * 2**20),
        cost_estimate=pl.CostEstimate(
            flops=2 * count * width * pieces * (double + middle),
            bytes_accessed=pieces * width * (double + middle) * 4 + count * width * 8,
            transcendentals=0,
        ),
        name="expert_grads",
    )(*operands)


def grads_kernel(*refs, plan, count):
    inputs, outs = refs[:-count], refs[-count:]
    rows = outs[0].shape[0]
    at = 0
    for width, starts in plan:
        left, right = [], []
        for start in starts:
            pair, inputs = inputs[:4], inputs[4:]
            left += [pair[0][...], pair[1][...]]
            right += [values[:, start : start + width] for values in pair[2:]]
        total = tn(jnp.concatenate(left, axis=0), jnp.concatenate(right, axis=0))
        for k, out in enumerate(outs):
            out[:, at : at + width] = total[k * rows : (k + 1) * rows].astype(BF16)
        at += width


def grads_of(segments, count):
    plan, operands, specs = [], [], []
    rows = segments[0][1][0][0].shape[1]

    def block(values, at, width):
        return pl.BlockSpec((values.shape[0], width), lambda _: (0, at // width))

    flops = 0
    for width, products in segments:
        starts = []
        for left_mine, left_other, right_mine, right_other, at in products:
            operands += [left_mine, left_other, right_mine, right_other]
            whole = at % width > 0
            starts.append(at if whole else 0)
            specs += [block(left_mine, 0, rows)] * 2
            specs += [block(right_mine, 0 if whole else at, right_mine.shape[1] if whole else width)] * 2
            flops += 4 * rows * width * left_mine.shape[0]
        plan.append((width, tuple(starts)))
    total = sum(width for width, _ in segments)
    return pl.pallas_call(
        functools.partial(grads_kernel, plan=tuple(plan), count=count),
        grid=(1,),
        in_specs=specs,
        out_specs=[pl.BlockSpec((rows // count, total), lambda _: (0, 0))] * count,
        out_shape=[jax.ShapeDtypeStruct((rows // count, total), BF16)] * count,
        compiler_params=pltpu.CompilerParams(vmem_limit_bytes=60 * 2**20),
        cost_estimate=pl.CostEstimate(
            flops=flops, bytes_accessed=4 * rows * total, transcendentals=0
        ),
    )(*operands)


def swap_halves(values):
    width = values.shape[1]
    lane = lax.broadcasted_iota(jnp.int32, values.shape, 1)
    return jnp.where(
        lane % ROPE < ROPE // 2,
        pltpu.roll(values, width - ROPE // 2, 1),
        pltpu.roll(values, ROPE // 2, 1),
    )


def repeated(table, times):
    return jnp.concatenate([table] * times, axis=1)


def upper_lanes(shape, head):
    return lax.broadcasted_iota(jnp.int32, shape, 1) // ROPE == head % 2


def lefts_and_rights(block, half, into):
    rows, width = block.shape
    if half % 16 == 0:
        cut = block.reshape(rows // (2 * half), 2 * half, width)
        return [
            cut[:, side * half : (side + 1) * half].reshape(rows // 2, width) for side in range(into)
        ]
    out = []
    for side in range(into):
        shape = (rows // 2, rows)
        row = lax.broadcasted_iota(jnp.int32, shape, 0)
        column = lax.broadcasted_iota(jnp.int32, shape, 1)
        wanted = row // half * (2 * half) + side * half + row % half
        out.append(nn((column == wanted).astype(BF16), block).astype(BF16))
    return out


def attention_kernel(
    hidden,
    mask,
    cosine,
    sine,
    weights,
    normed_two,
    mixed_out,
    normed_one_out,
    latent_norm_out,
    latent_in_out,
    latent_scale_out,
    query_out,
    key_value_out,
    rope_key_out,
    probs_out,
    head_out,
    gains_out,
    ups_out,
    first,
    output,
    up,
    sems,
    *,
    half,
):
    first_width, output_width = first.shape[1], output.shape[1]
    copies = [
        pltpu.make_async_copy(weights.at[:, pl.ds(at, target.shape[1])], target, sems.at[i])
        for i, (at, target) in enumerate(
            ((0, first), (first_width + output_width, up), (first_width, output))
        )
    ]
    for copy in copies:
        copy.start()
    hidden_wide = hidden[...].astype(F32)
    norm_one = hidden_wide * inverse_rms(hidden_wide)
    copies[0].wait()
    tail = first[:, first_width - 128 :]
    picked = lax.broadcasted_iota(jnp.int32, (16, 128), 1) == ROPE + lax.broadcasted_iota(
        jnp.int32, (16, 128), 0
    )
    picked = picked.astype(BF16)
    gains = nt(picked, tail)
    latent_gains = nt(picked, lefts_and_rights(tail, half, 1)[0])
    gains_out[...] = jnp.concatenate(
        [gains[:2], jnp.concatenate([latent_gains[2:3], jnp.zeros((1, D - RANK), F32)], axis=1),
         jnp.zeros((5, D), F32)], axis=0
    )
    normed_one = (norm_one * gains[0:1]).astype(BF16)
    normed_one_out[...] = normed_one
    projected = nn(normed_one, first[...])
    nope_width = H * NOPE
    query_width = H * (NOPE + ROPE)
    latent_part = projected[:, query_width : query_width + RANK]
    latent_scale = inverse_rms(latent_part)
    latent_norm = latent_part * latent_scale
    latent_in = (latent_norm * latent_gains[2:3]).astype(BF16)
    latent_norm_out[...] = latent_norm
    latent_in_out[...] = latent_in
    latent_scale_out[...] = jnp.broadcast_to(latent_scale, latent_scale_out.shape)
    cos, sin = cosine[...], sine[...]
    rope = projected[:, nope_width:query_width]
    rope = rope * repeated(cos, H // 2) + swap_halves(rope) * repeated(sin, H // 2)
    query_out[:, :nope_width] = projected[:, :nope_width].astype(BF16)
    query_out[:, nope_width:] = rope.astype(BF16)
    key = projected[:, query_width + RANK : query_width + RANK + 128]
    key = jnp.where(upper_lanes(key.shape, 0), key, 0.0)
    key = key + pltpu.roll(key, ROPE, 1)
    rope_key = (key * cos + swap_halves(key) * sin).astype(BF16)
    rope_key_out[...] = rope_key
    copies[1].wait()
    for side, part in enumerate(lefts_and_rights(up[...], half, 2)):
        ups_out[side] = part
        key_value_out[:, side * UW : (side + 1) * UW] = nn(latent_in, part).astype(BF16)
    scaling = (NOPE + ROPE) ** (-0.5)
    allowed = mask[...]
    for head in range(H):
        pair = query_out[:, nope_width + head // 2 * 128 : nope_width + head // 2 * 128 + 128]
        pair = jnp.where(upper_lanes(pair.shape, head), pair, jnp.zeros_like(pair))
        query = jnp.concatenate([query_out[:, head * NOPE : (head + 1) * NOPE], pair], axis=1)
        at = head * (NOPE + VDIM)
        keys = jnp.concatenate([key_value_out[:, at : at + NOPE], rope_key], axis=1)
        scores = nt(query, keys) * scaling
        raised = jnp.exp(scores) * allowed
        probs = raised / jnp.sum(raised, axis=-1, keepdims=True)
        probs_out[head] = probs
        head_out[:, head * VDIM : (head + 1) * VDIM] = nn(
            probs.astype(BF16), key_value_out[:, at + NOPE : at + NOPE + VDIM]
        ).astype(BF16)
    copies[2].wait()
    mixed = hidden_wide + nt(head_out[...], output[...])
    mixed_out[...] = mixed
    normed_two[...] = (mixed * inverse_rms(mixed) * gains[1:2]).astype(BF16)


def attention(hidden, mask, cosine, sine, weights, half):
    rows, width = hidden.shape
    query_width = H * (NOPE + ROPE)
    first_width = query_width + RANK + 128
    vmem = pl.BlockSpec(memory_space=pltpu.VMEM)
    shapes = [
        ((rows, width), BF16),
        ((rows, width), F32),
        ((rows, width), BF16),
        ((rows, RANK), F32),
        ((rows, RANK), BF16),
        ((rows, 128), F32),
        ((rows, query_width), BF16),
        ((rows, 2 * UW), BF16),
        ((rows, 128), BF16),
        ((H, rows, rows), F32),
        ((rows, H * VDIM), BF16),
        ((8, width), F32),
        ((2, RANK, UW), BF16),
    ]
    return pl.pallas_call(
        functools.partial(attention_kernel, half=half),
        in_specs=[vmem] * 4 + [pl.BlockSpec(memory_space=pl.ANY)],
        out_specs=[vmem] * len(shapes),
        out_shape=[jax.ShapeDtypeStruct(shape, dtype) for shape, dtype in shapes],
        scratch_shapes=[
            pltpu.VMEM((width, first_width), BF16),
            pltpu.VMEM((width, H * VDIM), BF16),
            pltpu.VMEM((width, UW), BF16),
            pltpu.SemaphoreType.DMA((3,)),
        ],
        compiler_params=pltpu.CompilerParams(vmem_limit_bytes=60 * 2**20),
        cost_estimate=pl.CostEstimate(
            flops=2 * rows * width * (first_width + 3 * width),
            bytes_accessed=2 * width * (first_width + 2 * width) + 8 * rows * width,
            transcendentals=H * rows * rows,
        ),
        name="attention",
    )(hidden, mask, cosine, sine, weights)


def mixed_back_kernel(*refs):
    count = (len(refs) - 7) // 2
    shared_dx, out_grad, mixed, gains = refs[:4]
    selectors, back = refs[4 : 4 + count], refs[4 + count : 4 + 2 * count]
    grad_mixed_out, mixed_low, gain_out = refs[4 + 2 * count :]
    grad = shared_dx[...]
    for selector, rows in zip(selectors, back):
        grad = grad + tn(selector[...], rows[...])
    scale = inverse_rms(mixed[...])
    norm_two = mixed[...] * scale
    gain_out[...] = jnp.broadcast_to(jnp.sum(grad * norm_two, axis=0, keepdims=True), gain_out.shape)
    grad_norm = grad * gains[1:2]
    grad_mixed = out_grad[...].astype(F32) + scale * (
        grad_norm - norm_two * jnp.mean(grad_norm * norm_two, axis=-1, keepdims=True)
    )
    grad_mixed_out[...] = grad_mixed
    mixed_low[...] = grad_mixed.astype(BF16)


def mixed_back(shared_dx, out_grad, mixed, gains, selectors, back):
    rows, width = mixed.shape
    vmem = pl.BlockSpec(memory_space=pltpu.VMEM)
    total = sum(values.shape[0] for values in back)
    return pl.pallas_call(
        mixed_back_kernel,
        in_specs=[vmem] * (4 + 2 * len(back)),
        out_specs=[vmem] * 3,
        out_shape=[
            jax.ShapeDtypeStruct((rows, width), F32),
            jax.ShapeDtypeStruct((rows, width), BF16),
            jax.ShapeDtypeStruct((8, width), F32),
        ],
        compiler_params=pltpu.CompilerParams(vmem_limit_bytes=60 * 2**20),
        cost_estimate=pl.CostEstimate(
            flops=2 * rows * width * total, bytes_accessed=2 * total * width, transcendentals=0
        ),
        name="mixed_back",
    )(shared_dx, out_grad, mixed, gains, *selectors, *back)


def attention_back_kernel(
    hidden,
    grad_mixed,
    mixed_low,
    cosine,
    sine,
    latent_norm,
    latent_scale,
    query,
    key_value,
    rope_key,
    probs,
    head_out,
    gains,
    ups,
    weights,
    back,
    input_grad,
    gain_out,
    first,
    output,
    sems,
):
    first_width = first.shape[1]
    grad_projected = back.at[:, 2 * UW :]
    grad_key_value = back.at[:, : 2 * UW]
    copies = [
        pltpu.make_async_copy(weights.at[:, pl.ds(at, target.shape[1])], target, sems.at[i])
        for i, (at, target) in enumerate(((first_width, output), (0, first)))
    ]
    for copy in copies:
        copy.start()
    copies[0].wait()
    rows = hidden.shape[0]
    nope_width = H * NOPE
    query_width = H * (NOPE + ROPE)
    scaling = (NOPE + ROPE) ** (-0.5)
    heads = nn(mixed_low[...], output[...]).astype(BF16)
    rope_sum = jnp.zeros((rows, 128), F32)
    rope_grads = []
    for head in range(H):
        grad_head = heads[:, head * VDIM : (head + 1) * VDIM]
        at = head * (NOPE + VDIM)
        weights_here = probs[head]
        own_lanes = upper_lanes((rows, 128), head)
        pair = query[:, nope_width + head // 2 * 128 : nope_width + head // 2 * 128 + 128]
        pair = jnp.where(own_lanes, pair, jnp.zeros_like(pair))
        query_here = jnp.concatenate([query[:, head * NOPE : (head + 1) * NOPE], pair], axis=1)
        keys = jnp.concatenate([key_value[:, at : at + NOPE], rope_key[...]], axis=1)
        grad_probs = nt(grad_head, key_value[:, at + NOPE : at + NOPE + VDIM])
        delta = jnp.sum(
            grad_head.astype(F32) * head_out[:, head * VDIM : (head + 1) * VDIM].astype(F32),
            axis=-1,
            keepdims=True,
        )
        grad_scores = (weights_here * (grad_probs - delta) * scaling).astype(BF16)
        grad_query = nn(grad_scores, keys)
        grad_projected[:, head * NOPE : (head + 1) * NOPE] = grad_query[:, :NOPE].astype(BF16)
        rope_grads.append(jnp.where(own_lanes, grad_query[:, NOPE:], 0.0))
        grad_keys = tn(grad_scores, query_here)
        rope_sum = rope_sum + grad_keys[:, NOPE:]
        grad_key_value[:, at : at + NOPE] = grad_keys[:, :NOPE].astype(BF16)
        grad_key_value[:, at + NOPE : at + NOPE + VDIM] = tn(
            weights_here.astype(BF16), grad_head
        ).astype(BF16)
    cos, sin = cosine[...], sine[...]
    rope = jnp.concatenate(
        [rope_grads[2 * pair] + rope_grads[2 * pair + 1] for pair in range(H // 2)], axis=1
    )
    rope = rope * repeated(cos, H // 2) - swap_halves(rope) * repeated(sin, H // 2)
    grad_projected[:, nope_width:query_width] = rope.astype(BF16)
    key = rope_sum + pltpu.roll(rope_sum, ROPE, 1)
    key = key * cos - swap_halves(key) * sin
    key = jnp.where(upper_lanes(key.shape, 0), key, 0.0)
    grad_projected[:, query_width + RANK :] = key.astype(BF16)
    grad_latent_in = nt(grad_key_value[:, :UW], ups[0]) + nt(grad_key_value[:, UW:], ups[1])
    norm = latent_norm[...]
    latent_gain_grad = jnp.sum(grad_latent_in * norm, axis=0, keepdims=True)
    grad_norm = grad_latent_in * gains[2:3, :RANK]
    grad_latent = latent_scale[:, 0:1] * (
        grad_norm - norm * jnp.mean(grad_norm * norm, axis=-1, keepdims=True)
    )
    grad_projected[:, query_width : query_width + RANK] = grad_latent.astype(BF16)
    copies[1].wait()
    grad_normed = nt(grad_projected[...], first[...])
    hidden_wide = hidden[...].astype(F32)
    scale = inverse_rms(hidden_wide)
    norm_one = hidden_wide * scale
    gain_out[...] = jnp.concatenate(
        [
            jnp.sum(grad_normed * norm_one, axis=0, keepdims=True),
            jnp.concatenate([latent_gain_grad, jnp.zeros((1, D - RANK), F32)], axis=1),
            jnp.zeros((6, D), F32),
        ],
        axis=0,
    )
    grad_norm = grad_normed * gains[0:1]
    input_grad[...] = grad_mixed[...] + scale * (
        grad_norm - norm_one * jnp.mean(grad_norm * norm_one, axis=-1, keepdims=True)
    )


def attention_back(operands, weights):
    hidden = operands[0]
    rows, width = hidden.shape
    first_width = H * (NOPE + ROPE) + RANK + 128
    vmem = pl.BlockSpec(memory_space=pltpu.VMEM)
    return pl.pallas_call(
        attention_back_kernel,
        in_specs=[vmem] * len(operands) + [pl.BlockSpec(memory_space=pl.ANY)],
        out_specs=[vmem] * 3,
        out_shape=[
            jax.ShapeDtypeStruct((rows, first_width + 2 * UW), BF16),
            jax.ShapeDtypeStruct((rows, width), F32),
            jax.ShapeDtypeStruct((8, width), F32),
        ],
        scratch_shapes=[
            pltpu.VMEM((width, first_width), BF16),
            pltpu.VMEM((width, H * VDIM), BF16),
            pltpu.SemaphoreType.DMA((2,)),
        ],
        compiler_params=pltpu.CompilerParams(vmem_limit_bytes=60 * 2**20),
        cost_estimate=pl.CostEstimate(
            flops=2 * rows * width * (first_width + 3 * width),
            bytes_accessed=2 * width * (first_width + 2 * width) + 8 * rows * width,
            transcendentals=0,
        ),
        name="attention_back",
    )(*operands, weights)


def after_kernel(values, late, out):
    pass


def after(values, late):
    anywhere = pl.BlockSpec(memory_space=pl.ANY)
    return pl.pallas_call(
        after_kernel,
        in_specs=[anywhere, anywhere],
        out_specs=anywhere,
        out_shape=jax.ShapeDtypeStruct(values.shape, values.dtype),
        input_output_aliases={0: 0},
        cost_estimate=pl.CostEstimate(flops=0, bytes_accessed=0, transcendentals=0),
        name="after",
    )(values, late)


def axes_of(devices):
    return {32: ((8, 4), (4, 2), (2, 2)), 128: ((32, 4), (8, 4), (2, 4))}[devices]


def swap_with(values, devices, offset):
    return lax.ppermute(values, "fsdp", [(i, i ^ offset) for i in range(devices)])


def pick(values, index, axis):
    return lax.dynamic_index_in_dim(values, index, axis, keepdims=False)


def row_order(devices, axis, half=None):
    me = lax.axis_index("fsdp")
    own = D // devices
    axes = axes_of(devices)
    to = jnp.arange(D, dtype=jnp.int32)
    chip_row = to % (D // 2)
    stride, size = axes[axis]
    block = chip_row // (D // 2 // size)
    rest = chip_row % (D // 2 // size) // own
    device = (me % 2) ^ (to // (D // 2))
    device = device + (((me // stride) % size) ^ block) * stride
    for other in (2, 1, 0):
        if other != axis:
            device = device + rest % axes[other][1] * axes[other][0]
            rest = rest // axes[other][1]
    row = to % own
    if half is None:
        source = device * own + row
        return (jnp.arange(D, dtype=jnp.int32)[:, None] == source[None, :]).astype(BF16)
    source = device * half + row % half
    hit = jnp.arange(D // 2, dtype=jnp.int32)[:, None] == source[None, :]
    return [(hit & (row // half == side)[None, :]).astype(BF16) for side in range(2)]


def scatter_sum(blocks, devices, order, late=None):
    me = lax.axis_index("fsdp")
    axes = axes_of(devices)
    left = [0, 1, 2]
    values = None
    for axis in order:
        stride, size = axes[axis]
        at = left.index(axis)
        left.remove(axis)
        mine = (me // stride) % size
        if values is not None:
            blocks = [pick(values, mine ^ k, at) for k in range(size)]
        total = blocks[0] if late is None or values is not None else after(blocks[0], late)
        total = total.astype(F32)
        parts = [swap_with(blocks[k], devices, k * stride) for k in range(1, size)]
        for part in parts:
            total = total + part.astype(F32)
        values = total if not left else total.astype(BF16)
        if values.ndim == 2 and left:
            values = values.reshape(
                *(axes[other][1] for other in left), D // devices, values.shape[-1]
            )
    return values


def body(
    hidden_in,
    out_grad,
    doc_ids,
    routes,
    gate_values,
    attn_gain,
    query_proj,
    latent_proj,
    latent_gain,
    latent_up,
    output_proj,
    ffn_gain,
    shared_in,
    shared_out,
    expert_in,
    expert_out,
):
    devices = lax.axis_size("fsdp")
    rows_here = hidden_in.shape[0]
    own = D // devices
    half = own // 2

    along_x, along_y = row_order(devices, 2), row_order(devices, 1)
    sides_x, sides_y = row_order(devices, 2, half), row_order(devices, 1, half)

    def mine_and_other(columns, order):
        placed = matmul(columns, order).astype(BF16)
        return (placed[:, : D // 2], swap_with(placed[:, D // 2 :], devices, 1))

    spare = 128 - LW % 128
    query_width, output_width = query_proj.shape[1], output_proj.shape[1]
    gain_at = query_width + LW
    output_at = gain_at + spare
    by_head = query_proj.reshape(own, H, NOPE + ROPE)
    gathered = lax.all_gather(
        jnp.concatenate(
            [
                by_head[:, :, :NOPE].reshape(own, H * NOPE),
                by_head[:, :, NOPE:].reshape(own, H * ROPE),
                latent_proj,
                attn_gain[:, None],
                ffn_gain[:, None],
                jnp.concatenate([latent_gain, jnp.zeros_like(latent_gain)])[:, None],
                jnp.zeros((own, spare - 3), BF16),
                output_proj,
                jnp.concatenate([latent_up[:, :UW], latent_up[:, UW:]], axis=0),
            ],
            axis=1,
        ),
        "fsdp",
        axis=0,
        tiled=True,
    )
    gathered_shared = lax.all_gather(
        jnp.concatenate([shared_in, shared_out], axis=1), "fsdp", axis=0, tiled=True
    )

    per_device = expert_in.shape[0]
    pieces = 2 if per_device % 2 == 0 else 1
    units = 2 * EXPERTS // pieces
    local_units = units // devices
    token = jnp.arange(rows_here, dtype=jnp.int32)
    earlier = (token[None, :] < token[:, None]).astype(BF16)

    def routing(names, values, base, count):
        unit_expert = (base + jnp.arange(count, dtype=jnp.int32)) // (2 // pieces)
        named = names[:, :, None] == unit_expert[None, None, :]
        hits = jnp.any(named, axis=1)
        gates = jnp.sum(jnp.where(named, values[:, :, None], 0.0), axis=1)
        slots = matmul(earlier, hits.astype(BF16)).astype(jnp.int32)
        return (jnp.where(hits, slots, CAP).T, gates.T)

    slots, gates = routing(routes, gate_values, 0, units)
    chosen = slots[:, None, :] == jnp.arange(CAP, dtype=jnp.int32)[None, :, None]
    gate_wide = jnp.where(chosen, gates[:, None, :], 0.0).reshape(units * CAP, rows_here)
    gate_rows = jnp.sum(gate_wide, axis=-1, keepdims=True)
    selector = chosen.astype(BF16)
    unit_selector = selector.reshape(devices, local_units, CAP, rows_here)
    unit_selector = [
        unit_selector[:, u].reshape(devices * CAP, rows_here) for u in range(local_units)
    ]
    selector = selector.reshape(units * CAP, rows_here)

    def exchange(rows):
        return lax.all_to_all(rows, "fsdp", split_axis=0, concat_axis=0, tiled=True)

    def exchange_unit(rows):
        return exchange(rows.reshape(devices, CAP, D)).reshape(devices * CAP, D)

    grad_rows = exchange(
        (gate_rows * matmul(selector, out_grad)).astype(BF16).reshape(devices, local_units * CAP, D)
    ).reshape(devices, local_units, CAP, D)
    grad_rows = [grad_rows[:, u].reshape(devices * CAP, D) for u in range(local_units)]

    allowed, cosine_table, sine_table = tables(doc_ids[0])
    cosine_lanes = jnp.concatenate([cosine_table] * 4, axis=1)
    sine_lanes = jnp.concatenate([-sine_table, sine_table] * 2, axis=1)
    (
        normed_two,
        mixed,
        normed_one,
        latent_norm,
        latent_in,
        latent_scale,
        queries,
        key_values,
        rope_key,
        probs,
        head_out,
        gain_rows,
        ups,
    ) = attention(hidden_in, allowed.astype(F32), cosine_lanes, sine_lanes, gathered, half)

    rows_out = [matmul(unit_selector[u], normed_two).astype(BF16) for u in range(local_units)]
    rows_in = []
    for rows in rows_out:
        rows_in.append(exchange_unit(rows))

    sent_dx, back_dx, back_out, saved = [], [], [], []
    for u in range(local_units):
        dx_rows, y_rows, activation, grad_pre = experts(
            rows_in[u], grad_rows[u], expert_in, expert_out, u, pieces
        )
        sent_dx.append(dx_rows)
        back_dx.append(exchange_unit(dx_rows))
        back_out.append(y_rows.reshape(devices, CAP, D))
        saved.append((activation, grad_pre))
    shared_rows = normed_two
    for rows in sent_dx:
        shared_rows = after(shared_rows, rows)
    shared_width = shared_in.shape[1]
    full_shared_in = gathered_shared[:, :shared_width]
    full_shared_out = gathered_shared[:, shared_width:]
    shared_pre = matmul(shared_rows, full_shared_in)
    shared_act = swiglu_forward(shared_pre)
    grad_shared_act = matmul(out_grad, full_shared_out)
    grad_shared_pre = swiglu_backward(shared_pre, grad_shared_act)
    middle = shared_out.shape[1]
    dpre_pair = (grad_shared_pre, swap_with(grad_shared_pre, devices, 1))
    act_pair = (shared_act, swap_with(shared_act, devices, 1))
    size_x, size_y = axes_of(devices)[2][1], axes_of(devices)[1][1]
    blocks_x = grads_of(
        (
            (middle, ((*mine_and_other(normed_two, along_x), *dpre_pair, 0),)),
            (middle, ((*mine_and_other(out_grad, along_x), *act_pair, 0),)),
        ),
        size_x,
    )
    blocks_y = grads_of(
        ((middle, ((*mine_and_other(normed_two, along_y), *dpre_pair, middle),)),), size_y
    )
    shared_blocks = (blocks_x, blocks_y)
    shared_y = product("tf,df->td", shared_act, full_shared_out)
    shared_dx = product("tf,df->td", grad_shared_pre, full_shared_in)

    back_out = jnp.concatenate(back_out, axis=1)
    for rows in back_dx:
        back_out = after(back_out, rows)
    back_out = exchange(back_out).reshape(units * CAP, D)

    grad_mixed, mixed_low, ffn_gain_grad = mixed_back(
        shared_dx, out_grad, mixed, gain_rows, unit_selector, back_dx
    )

    heads_pair = (head_out, swap_with(head_out, devices, 1))
    first_left = mine_and_other(normed_one, along_y)
    up_left = [mine_and_other(latent_in, side) for side in sides_x]
    output_left = mine_and_other(mixed_low, along_x)
    back, input_grad, other_gain_grads = attention_back(
        (
            hidden_in,
            grad_mixed,
            mixed_low,
            cosine_lanes,
            sine_lanes,
            latent_norm,
            latent_scale,
            queries,
            key_values,
            rope_key,
            probs,
            head_out,
            gain_rows,
            ups,
        ),
        gathered,
    )
    back_pair = (back, swap_with(back, devices, 1))
    gain_grads = jnp.concatenate(
        [other_gain_grads[:1], ffn_gain_grad[:1], jnp.zeros((6, D), F32)], axis=0
    ).astype(BF16)
    placed = matmul(gain_grads, along_y) + jnp.pad(
        matmul(other_gain_grads[1:7, :RANK].astype(BF16), sides_y[0]), ((2, 0), (0, 0))
    )
    placed = placed.astype(BF16)
    gain_left = (placed[:, : D // 2], swap_with(placed[:, D // 2 :], devices, 1))
    row = jnp.arange(8, dtype=jnp.int32)[:, None]
    lane = jnp.arange(output_at, dtype=jnp.int32)[None, :]
    gain_right = ((row < 3) & (lane == gain_at + row)).astype(BF16)
    blocks_y = grads_of(
        (
            (
                output_at,
                ((*first_left, *back_pair, 2 * UW), (*gain_left, gain_right, gain_right, 0)),
            ),
        ),
        size_y,
    )
    owned_first = scatter_sum(blocks_y, devices, (1, 2, 0))
    blocks_x = grads_of(
        (
            (output_width, ((*output_left, *heads_pair, 0),)),
            (UW, tuple((*up_left[i], *back_pair, i * UW) for i in range(2))),
        ),
        size_x,
    )
    owned_second = scatter_sum(blocks_x, devices, (2, 1, 0))
    owned_gate_out = scatter_sum(shared_blocks[0], devices, (2, 1, 0), blocks_x[0])
    owned_up_in = scatter_sum(shared_blocks[1], devices, (1, 2, 0), blocks_x[0])
    owned_output, owned_up = owned_second[:, :output_width], owned_second[:, output_width:]
    gates_high = lax.reduce_precision(gate_wide, 8, 7)
    gates_low = (gate_wide - gates_high).astype(BF16)
    back_out = after(back_out, blocks_x[0])
    routed_y = product("rt,rd->td", gates_high.astype(BF16), back_out) + product(
        "rt,rd->td", gates_low, back_out
    )
    layer_out = (mixed + shared_y + routed_y).astype(BF16)
    held = None
    for u in range(local_units):
        held = expert_grads(
            rows_in[u], grad_rows[u], *saved[u], per_device, u, blocks_x[-1] if u else None, held
        )
    owned_query = jnp.concatenate(
        [
            owned_first[:, : H * NOPE].reshape(own, H, NOPE),
            owned_first[:, H * NOPE : query_width].reshape(own, H, ROPE),
        ],
        axis=2,
    ).reshape(own, query_width)
    return (
        layer_out,
        input_grad,
        owned_first[:, gain_at],
        owned_query,
        owned_first[:, query_width:gain_at],
        owned_first[:half, gain_at + 2],
        jnp.concatenate([owned_up[:half], owned_up[half:]], axis=1),
        owned_output,
        owned_first[:, gain_at + 1],
        jnp.concatenate([owned_gate_out[:, :middle], owned_up_in], axis=1),
        owned_gate_out[:, middle:],
        held[0],
        held[1],
    )


def solution(mesh):
    rows = P("fsdp", None)
    flat = P("fsdp")
    cube = P("fsdp", None, None)
    in_specs = (rows,) * 5 + (flat, rows, rows, flat, rows, rows, flat, rows, rows, cube, cube)
    out_specs = (rows, rows, flat, rows, rows, flat, rows, rows, flat, rows, rows, cube, cube)
    return jax.shard_map(body, mesh=mesh, in_specs=in_specs, out_specs=out_specs, check_vma=False)
```

time: 568 us -> 476 us (0.84)
  matrix products: 138 us -> 30.7 us
  Pallas kernels: 0 us -> 99.2 us
  local copies, waits for them, and re-layouts: 69.9 us -> 27.9 us
  other arithmetic: 57.8 us -> 19.3 us
  starting transfers between devices: 35 us -> 56 us
  waiting for transfers between devices: 241 us -> 220 us
    dot_general x38 -> x4, matrix products: 116 us -> 9.83 us  [product(): jnp.einsum(pattern, left_side, right_side, preferred_element_type=F32)]
    pallas_call x0 -> x18, Pallas kernels: none -> 99.2 us  [the longest x2 35 us: experts(): pl.pallas_call(experts_kernel, grid=(count // block, pieces), in_specs=[r...]
    ppermute x0 -> x32, waiting for transfers between devices: none -> 70.7 us  [swap_with(): lax.ppermute(values, 'fsdp', [(i, i ^ offset) for i in range(devices)])]
    all_gather x1, waiting for transfers between devices: 60.6 us -> 0.01 us  [body(): lax.all_gather(jnp.concatenate([shared_in, shared_out], axis=1), 'fsdp',...]
    reduce_scatter x2 -> x0, waiting for transfers between devices: 30.4 us -> none  [the longest x1 30.4 us: body(): lax.psum_scatter(grad_packed, 'fsdp', scatter_dimension=0, tiled=True)]
    concatenate x5, other arithmetic: 33 us -> 3.29 us  [the longest x1 1.63 us: body(): back_out = jnp.concatenate(back_out, axis=1)]
    ppermute x0 -> x32, starting transfers between devices: none -> 28.2 us  [swap_with(): lax.ppermute(values, 'fsdp', [(i, i ^ offset) for i in range(devices)])]
    unnamed x139 -> x71, local copies, waits for them, and re-layouts: 30.2 us -> 7.66 us
  transfers between devices with their start and end apart: 12 -> 40, of which waited for: 8 -> 17; matrix products, arithmetic and copies ran while one was open for 44% -> 13% of each run, Pallas kernels for 0% -> 21%
where the time goes in v2:
time: 476 us; the launch traced here: 469 us
  waiting for transfers between devices  220 us (46%)
  Pallas kernels  99.2 us (21%)
  starting transfers between devices  56 us (12%)
  matrix products  30.7 us (6%)
  local copies, waits for them, and re-layouts  27.9 us (6%)
  other arithmetic  19.3 us (4%)
  between operations  15.1 us (3%)
    all_gather x1, waiting for transfers between devices, body(): lax.all_gather(jnp.concatenate([by_head[:, :, :NOPE].reshape(own, H * NOP...  88.4 us
    ppermute x32, waiting for transfers between devices, swap_with(): lax.ppermute(values, 'fsdp', [(i, i ^ offset) for i in range(devices)])  70.7 us
    all_to_all x6, waiting for transfers between devices, exchange(): return lax.all_to_all(rows, 'fsdp', split_axis=0, concat_axis=0, tiled=True)  61.1 us
    pallas_call x2, Pallas kernels, experts(): pl.pallas_call(experts_kernel, grid=(count // block, pieces), in_specs=[r...  35 us
    ppermute x32, starting transfers between devices, swap_with(): lax.ppermute(values, 'fsdp', [(i, i ^ offset) for i in range(devices)])  28.2 us
    all_to_all x6, starting transfers between devices, exchange(): return lax.all_to_all(rows, 'fsdp', split_axis=0, concat_axis=0, tiled=True)  27.8 us
    pallas_call x2, Pallas kernels, expert_grads(): pl.pallas_call(expert_grads_kernel, grid=(pieces, width // chunk), in_spe...  26.8 us
    dot_general x15, matrix products, matmul(): return jnp.dot(left_side, right_side, preferred_element_type=F32)  20.9 us
  transfers between devices with their start and end apart: 40, of which 17 were waited for; matrix products, arithmetic and copies ran while one was open for 13% of the time, Pallas kernels for 21%

profile of v2, /device:TPU:0, one launch (start us, length us, event | category | flops | bytes accessed | tf_op | source)
XLA Modules:
  0.0 468.5 jit_solution(13123443875782438174)
XLA Ops:
  11.6 1.7 concatenate.42
  13.3 1.7 pad_maximum_fusion.3
  15.9 2.0 multiply_convert_fusion
  17.9 7.3 %all-to-all-start.1 = ((bf16[32,32,1024]{2,1,0:T(8,128)(2,1)}), bf16[32,32,1024]{2,1,0:T(8,128)(2,1)S(1)}, u32[]{:S(2)}, u32[]{:S(2)}) async-start(bf16[32,32,1024]{2,1,0:T(8,128)(2,1)} %bitcast.146), calls=%async_computation.1 | async-start | bytes 4194304 | tf_op jit(solution)/shard_map/all_to_all | solution.py:764
  29.4 88.4 %all-gather.3.cloned.1.call-done.weights = bf16[1024,4224]{1,0:T(8,128)(2,1)} async-done(((bf16[32,4224]{1,0:T(8,128)(2,1)}), bf16[1024,4224]{1,0:T(8,128)(2,1)}) %all-gather.3.cloned.1.call-update) | async-done | bytes 8650768 | tf_op jit(solution)/shard_map/all_gather | solution.py:714
  117.7 9.0 %attention.1 = (bf16[128,1024]{1,0:T(8,128)(2,1)}, f32[128,1024]{1,0:T(8,128)}, bf16[128,1024]{1,0:T(8,128)(2,1)}, f32[128,512]{1,0:T(8,128)}, bf16[128,512]{1,0...) custom-call(bf16[128,1024]{1,0:T(8,128)(2,1)} %hidden.3, ...), custom_call_target="tpu_custom_call" | custom-call | flops 1375731712 | bytes 9699328 | tf_op jit(solution)/shard_map/attention/pallas_call | solution.py:409
  126.7 2.4 convolution_convert_fusion.1
  129.1 3.4 all-to-all-start
  137.9 35.2 %all-to-all-done = bf16[32,16,1024]{2,1,0:T(8,128)(2,1)} async-done(((bf16[32,16,1024]{2,1,0:T(8,128)(2,1)}), bf16[32,16,1024]{2,1,0:T(8,128)(2,1)}, u32[]{:S(2)}, u32[]{:S(2)}) %all-to-all-start) | async-done | bytes 1048608 | tf_op jit(solution)/shard_map/all_to_all | solution.py:764
  173.1 4.1 all-to-all-start.2
  182.1 17.5 %experts.2 = (bf16[512,1024]{1,0:T(8,128)(2,1)}, bf16[512,1024]{1,0:T(8,128)(2,1)}, bf16[2,512,704]{2,1,0:T(8,128)(2,1)}, bf16[2,512,1408]{2,1,0:T(8,128)(2,1)}) custom-call(bf16[512,1024]{1,0:T(8,128)(2,1)} %bitcast.8.rows, bf16[512,1024]{1,0:T(8,128)(2,1)} %bitcast.160, bf16[4,1024,1408]{2,1,0:T(8,128)(2,1)} %w_in.3, bf16[4,704,1024]{2,1,0:T(8,128)(2,1)} %w_out.3), custom_call_target="tpu_custom_call" | custom-call | flops 8858370048 | bytes 17170432 | tf_op jit(solution)/shard_map/experts/pallas_call | solution.py:128
  199.6 25.5 %all-to-all-done.2 = bf16[32,16,1024]{2,1,0:T(8,128)(2,1)S(1)} async-done(((bf16[32,16,1024]{2,1,0:T(8,128)(2,1)}), bf16[32,16,1024]{2,1,0:T(8,128)(2,1)S(1)}, u32[]{:S(2)}, u32[]{:S(2)}) %all-to-all-start.2) | async-done | bytes 1048608 | tf_op jit(solution)/shard_map/all_to_all | solution.py:764
  225.1 3.8 all-to-all-start.3
  232.4 17.5 %experts.3 = (bf16[512,1024]{1,0:T(8,128)(2,1)}, bf16[512,1024]{1,0:T(8,128)(2,1)}, bf16[2,512,704]{2,1,0:T(8,128)(2,1)}, bf16[2,512,1408]{2,1,0:T(8,128)(2,1)}) custom-call(bf16[512,1024]{1,0:T(8,128)(2,1)} %bitcast.151, bf16[512,1024]{1,0:T(8,128)(2,1)} %bitcast.155, bf16[4,1024,1408]{2,1,0:T(8,128)(2,1)} %w_in.3, bf16[4,704,1024]{2,1,0:T(8,128)(2,1)} %w_out.3), custom_call_target="tpu_custom_call" | custom-call | flops 8858370048 | bytes 17170432 | tf_op jit(solution)/shard_map/experts/pallas_call | solution.py:128
  249.9 4.8 %fusion.2 = f32[128,2816]{1,0:T(8,128)} fusion(bf16[128,1024]{1,0:T(8,128)(2,1)} %after.8, bf16[1024,4224]{1,0:T(8,128)(2,1)} %all-gather.5.cloned.1.call-done), kind=kOutput, calls=%fused_computation.2 | convolution fusion | flops 738197504 | bytes 7471104 | tf_op jit(solution)/shard_map/dot_general | solution.py:29
  255.1 5.3 %all-to-all-start.4 = ((bf16[32,16,1024]{2,1,0:T(8,128)(2,1)}), bf16[32,16,1024]{2,1,0:T(8,128)(2,1)S(1)}, u32[]{:S(2)}, u32[]{:S(2)}) async-start(bf16[32,16,1024]{2,1,0:T(8,128)(2,1)} %bitcast.23), calls=%async_computation.4 | async-start | bytes 2097152 | tf_op jit(solution)/shard_map/all_to_all | solution.py:764
  260.4 3.1 multiply_convert_fusion.2
  265.5 2.8 fusion.refs_0_
  268.3 13.3 %expert_grads.2 = (f32[4,1024,1408]{2,1,0:T(8,128)}, f32[4,704,1024]{2,1,0:T(8,128)}) custom-call(bf16[512,1024]{1,0:T(8,128)(2,1)} %bitcast.8.rows, bf16[512,1024]{1,0:T(8,128)(2,1)} %bitcast.161, bf16[2,512,704]{2,1,0:T(8,128)(2,1)} %get-tuple-element.85.act, bf16[2,512,1408]{2,1,0:T(8,128)(2,1)} %get-tuple-element.86.dpre), custom_call_target="tpu_custom_call" | custom-call | flops 4429185024 | bytes 21495808 | tf_op jit(solution)/shard_map/expert_grads/pallas_call | solution.py:187
  281.6 3.8 fusion.33
  285.5 1.6 pad_maximum_fusion.values
  287.6 2.9 shard_map.258
  290.5 1.8 collective-permute-start.27
  292.2 4.0 shard_map.257
  298.7 3.9 all-to-all-start.5
  302.7 3.6 mixed_back.1
  306.3 9.6 %attention_back.1 = (bf16[128,4224]{1,0:T(8,128)(2,1)}, f32[128,1024]{1,0:T(8,128)}, f32[8,1024]{1,0:T(8,128)}) custom-call(bf16[128,1024]{1,0:T(8,128)(2,1)} %hidden.3, f32[128,1024]{1,0:T(8,128)} %get-tuple-element.62.grad_mixed, bf16[128,1024]{1,0:T(8,128)(2,1)} %get-tuple-element.59.mixed_low, f32[128,128]{1,0:T(8,128)} %get-tuple-element.143.cosine, ...), custom_call_target="tpu_custom_call" | custom-call | flops 1375731712 | bytes 9699328 | tf_op jit(solution)/shard_map/attention_back/pallas_call | solution.py:577
  324.2 4.0 shard_map.255
  328.2 1.9 collective-permute-start.12
  330.8 4.5 shard_map.256
  340.0 6.8 %collective-permute-done.21 = bf16[256,2816]{1,0:T(8,128)(2,1)} collective-permute-done((bf16[256,2816]{1,0:T(8,128)(2,1)}, bf16[256,2816]{1,0:T(8,128)(2,1)}, u32[]{:S(2)}, u32[]{:S(2)}) %collective-permute-start.21) | collective-permute-done | bytes 1441824 | tf_op jit(solution)/shard_map/ppermute | solution.py:623
  346.8 1.7 add_convert_fusion
  350.1 13.5 %expert_grads.3 = (f32[4,1024,1408]{2,1,0:T(8,128)}, f32[4,704,1024]{2,1,0:T(8,128)}) custom-call(bf16[512,1024]{1,0:T(8,128)(2,1)} %bitcast.152, bf16[512,1024]{1,0:T(8,128)(2,1)} %bitcast.156, bf16[2,512,704]{2,1,0:T(8,128)(2,1)} %get-tuple-element.83.act, ...), custom_call_target="tpu_custom_call", output_to_operand_aliasing={{0}: (5, {}), {1}: (6, {})} | custom-call | flops 4429185024 | bytes 21495808 | tf_op jit(solution)/shard_map/expert_grads/pallas_call | solution.py:187
  363.6 19.0 %collective-permute-done.28 = bf16[4,32,1408]{2,1,0:T(8,128)(2,1)} collective-permute-done((bf16[4,32,1408]{2,1,0:T(8,128)(2,1)S(1)}, bf16[4,32,1408]{2,1,0:T(8,128)(2,1)}, u32[]{:S(2)}, u32[]{:S(2)}) %collective-permute-start.28) | collective-permute-done | bytes 360480 | tf_op jit(solution)/shard_map/ppermute | solution.py:623
  385.3 2.4 collective-permute-start.31
  389.2 2.0 collective-permute-start.23
  392.5 2.5 collective-permute-start.25
  395.0 2.8 collective-permute-done.30
  398.8 4.2 collective-permute-done.25
  403.0 7.7 %collective-permute-done.24 = bf16[32,2816]{1,0:T(8,128)(2,1)S(1)} collective-permute-done((bf16[32,2816]{1,0:T(8,128)(2,1)S(1)}, bf16[32,2816]{1,0:T(8,128)(2,1)S(1)}, u32[]{:S(2)}, u32[]{:S(2)}) %collective-permute-start.24) | collective-permute-done | bytes 180256 | tf_op jit(solution)/shard_map/ppermute | solution.py:623
  412.2 1.7 add_convert_fusion.2
  417.8 9.4 %collective-permute-done.13 = bf16[4,32,2048]{2,1,0:T(8,128)(2,1)S(1)} collective-permute-done((bf16[4,32,2048]{2,1,0:T(8,128)(2,1)S(1)}, bf16[4,32,2048]{2,1,0:T(8,128)(2,1)S(1)}, u32[]{:S(2)}, u32[]{:S(2)}) %collective-permute-start.13) | collective-permute-done | bytes 524320 | tf_op jit(solution)/shard_map/ppermute | solution.py:623
  427.4 1.7 collective-permute-start.16
  429.1 1.8 collective-permute-start.15
  433.8 2.9 collective-permute-done.14
  436.8 11.7 %collective-permute-done.15 = bf16[32,2048]{1,0:T(8,128)(2,1)S(1)} collective-permute-done((bf16[32,2048]{1,0:T(8,128)(2,1)S(1)}, bf16[32,2048]{1,0:T(8,128)(2,1)S(1)}, u32[]{:S(2)}, u32[]{:S(2)}) %collective-permute-start.15) | collective-permute-done | bytes 131104 | tf_op jit(solution)/shard_map/ppermute | solution.py:623
  449.9 2.9 collective-permute-done.10
  458.1 2.1 fusion.132
  (228 shorter events, 66.7 us)
Async XLA Ops:
  7.2 8.7 %copy-start.13 = (bf16[128,1024]{1,0:T(8,128)(2,1)S(1)}, bf16[128,1024]{1,0:T(8,128)(2,1)}, u32[]{:S(2)}) copy-start(bf16[128,1024]{1,0:T(8,128)(2,1)} %refs_1_.1) | copy-start | bytes 786436
  7.2 110.5 %all-gather.3.cloned.1.call-start = ((), (), s32[]{:S(2)}) async-start(), calls=%async_computation.6 | async-start | bytes 8921088 | tf_op jit(solution)/shard_map/all_gather | solution.py:714
  13.3 236.6 %all-gather.5.cloned.1.call-start = ((), (), s32[]{:S(2)}) async-start(), calls=%async_computation.7 | async-start | bytes 8921088 | tf_op jit(solution)/shard_map/all_gather | solution.py:733
  17.9 111.1 %all-to-all-start.1 = ((bf16[32,32,1024]{2,1,0:T(8,128)(2,1)}), bf16[32,32,1024]{2,1,0:T(8,128)(2,1)S(1)}, u32[]{:S(2)}, u32[]{:S(2)}) async-start(bf16[32,32,1024]{2,1,0:T(8,128)(2,1)} %bitcast.146), calls=%async_computation.1 | async-start | bytes 4194304 | tf_op jit(solution)/shard_map/all_to_all | solution.py:764
  26.9 263.6 %collective-permute-start.19 = (bf16[128,512]{1,0:T(8,128)(2,1)}, bf16[128,512]{1,0:T(8,128)(2,1)}, u32[]{:S(2)}, u32[]{:S(2)}) collective-permute-start(bf16[128,512]{1,0:T(8,128)(2,1)} %get-tuple-element.112), channel_id=1, source_target_pairs={{0,1},{1,0},{2,3},{3,2},{4,5},{5,4},{6,7},{7,6},{8,9},{9,8},{10,11... | collective-permute-start | bytes 393224 | tf_op jit(solution)/shard_map/ppermute | solution.py:623
  129.1 44.0 %all-to-all-start = ((bf16[32,16,1024]{2,1,0:T(8,128)(2,1)}), bf16[32,16,1024]{2,1,0:T(8,128)(2,1)}, u32[]{:S(2)}, u32[]{:S(2)}) async-start(bf16[32,16,1024]{2,1,0:T(8,128)(2,1)} %bitcast.7), calls=%async_computation | async-start | bytes 2097152 | tf_op jit(solution)/shard_map/all_to_all | solution.py:764
  173.1 52.0 %all-to-all-start.2 = ((bf16[32,16,1024]{2,1,0:T(8,128)(2,1)}), bf16[32,16,1024]{2,1,0:T(8,128)(2,1)S(1)}, u32[]{:S(2)}, u32[]{:S(2)}) async-start(bf16[32,16,1024]{2,1,0:T(8,128)(2,1)} %bitcast.15), calls=%async_computation.2 | async-start | bytes 2097152 | tf_op jit(solution)/shard_map/all_to_all | solution.py:764
  178.9 108.2 %collective-permute-start.26 = (bf16[128,512]{1,0:T(8,128)(2,1)}, bf16[128,512]{1,0:T(8,128)(2,1)}, u32[]{:S(2)}, u32[]{:S(2)}) collective-permute-start(bf16[128,512]{1,0:T(8,128)(2,1)} %get-tuple-element.116), channel_id=1, source_target_pairs={{0,1},{1,0},{2,3},{3,2},{4,5},{5,4},{6,7},{7,6},{8,9},{9,8},{10,11... | collective-permute-start | bytes 393224 | tf_op jit(solution)/shard_map/ppermute | solution.py:623
  199.6 31.0 %copy-start.32 = (bf16[128,1024]{1,0:T(8,128)(2,1)S(1)}, bf16[128,1024]{1,0:T(8,128)(2,1)}, u32[]{:S(2)}) copy-start(bf16[128,1024]{1,0:T(8,128)(2,1)} %get-tuple-element.73) | copy-start | bytes 786436
  225.1 30.0 %all-to-all-start.3 = ((bf16[32,16,1024]{2,1,0:T(8,128)(2,1)}), bf16[32,16,1024]{2,1,0:T(8,128)(2,1)S(1)}, u32[]{:S(2)}, u32[]{:S(2)}) async-start(bf16[32,16,1024]{2,1,0:T(8,128)(2,1)} %bitcast.157), calls=%async_computation.3 | async-start | bytes 2097152 | tf_op jit(solution)/shard_map/all_to_all | solution.py:764
  229.6 62.6 %collective-permute-start.17 = (bf16[128,512]{1,0:T(8,128)(2,1)}, bf16[128,512]{1,0:T(8,128)(2,1)}, u32[]{:S(2)}, u32[]{:S(2)}) collective-permute-start(bf16[128,512]{1,0:T(8,128)(2,1)} %get-tuple-element.114), channel_id=1, source_target_pairs={{0,1},{1,0},{2,3},{3,2},{4,5},{5,4},{6,7},{7,6},{8,9},{9,8},{10,11... | collective-permute-start | bytes 393224 | tf_op jit(solution)/shard_map/ppermute | solution.py:623
  255.1 8.4 %copy-start.4 = (bf16[32,16,1024]{2,1,0:T(8,128)(2,1)}, bf16[32,16,1024]{2,1,0:T(8,128)(2,1)S(1)}, u32[]{:S(2)}) copy-start(bf16[32,16,1024]{2,1,0:T(8,128)(2,1)S(1)} %all-to-all-done.3) | copy-start | bytes 3145732
  255.1 42.7 %all-to-all-start.4 = ((bf16[32,16,1024]{2,1,0:T(8,128)(2,1)}), bf16[32,16,1024]{2,1,0:T(8,128)(2,1)S(1)}, u32[]{:S(2)}, u32[]{:S(2)}) async-start(bf16[32,16,1024]{2,1,0:T(8,128)(2,1)} %bitcast.23), calls=%async_computation.4 | async-start | bytes 2097152 | tf_op jit(solution)/shard_map/all_to_all | solution.py:764
  263.5 18.1 %copy-start.31 = (bf16[128,1408]{1,0:T(8,128)(2,1)}, bf16[128,1408]{1,0:T(8,128)(2,1)S(1)}, u32[]{:S(2)}) copy-start(bf16[128,1408]{1,0:T(8,128)(2,1)S(1)} %get-tuple-element.97.refs_6_) | copy-start | bytes 1081348
  263.5 28.8 %collective-permute-start.20 = (bf16[128,1408]{1,0:T(8,128)(2,1)S(1)}, bf16[128,1408]{1,0:T(8,128)(2,1)}, u32[]{:S(2)}, u32[]{:S(2)}) collective-permute-start(bf16[128,1408]{1,0:T(8,128)(2,1)S(1)} %get-tuple-element.97.refs_6_), channel_id=1, source_target_pairs={{0,1},{1,0},{2,3},{3,2},{4,5},{5,4},{6,7},{7,6},{8,9},{9,8},{10,11... | collective-permute-start | bytes 1081352 | tf_op jit(solution)/shard_map/ppermute | solution.py:623
  263.9 23.5 %collective-permute-start.18 = (bf16[128,2816]{1,0:T(8,128)(2,1)S(1)}, bf16[128,2816]{1,0:T(8,128)(2,1)}, u32[]{:S(2)}, u32[]{:S(2)}) collective-permute-start(bf16[128,2816]{1,0:T(8,128)(2,1)S(1)} %pad_maximum_fusion.1.refs_2_), channel_id=1, source_target_pairs={{0,1},{1,0},{2,3},{3,2},{4,5},{5,4},{6,7},{7,6},{8,9},{9,8},{10,11... | collective-permute-start | bytes 2162696 | tf_op jit(solution)/shard_map/ppermute | solution.py:623
  268.3 13.3 %copy-start.20 = (f32[128,1024]{1,0:T(8,128)S(1)}, f32[128,1024]{1,0:T(8,128)}, u32[]{:S(2)}) copy-start(f32[128,1024]{1,0:T(8,128)} %get-tuple-element.52.refs_2_) | copy-start | bytes 1572868
  287.1 32.8 %collective-permute-start.2 = (bf16[128,512]{1,0:T(8,128)(2,1)}, bf16[128,512]{1,0:T(8,128)(2,1)}, u32[]{:S(2)}, u32[]{:S(2)}) collective-permute-start(bf16[128,512]{1,0:T(8,128)(2,1)} %get-tuple-element.124), channel_id=1, source_target_pairs={{0,1},{1,0},{2,3},{3,2},{4,5},{5,4},{6,7},{7,6},{8,9},{9,8},{10,11... | collective-permute-start | bytes 393224 | tf_op jit(solution)/shard_map/ppermute | solution.py:623
  287.4 34.1 %collective-permute-start.1 = (bf16[128,1024]{1,0:T(8,128)(2,1)S(1)}, bf16[128,1024]{1,0:T(8,128)(2,1)}, u32[]{:S(2)}, u32[]{:S(2)}) collective-permute-start(bf16[128,1024]{1,0:T(8,128)(2,1)S(1)} %copy-done.15), channel_id=1, source_target_pairs={{0,1},{1,0},{2,3},{3,2},{4,5},{5,4},{6,7},{7,6},{8,9},{9,8},{10,11... | collective-permute-start | bytes 786440 | tf_op jit(solution)/shard_map/ppermute | solution.py:623
  290.5 46.2 %collective-permute-start.27 = (bf16[256,1408]{1,0:T(8,128)(2,1)}, bf16[256,1408]{1,0:T(8,128)(2,1)}, u32[]{:S(2)}, u32[]{:S(2)}) collective-permute-start(bf16[256,1408]{1,0:T(8,128)(2,1)} %get-tuple-element.82), channel_id=1, source_target_pairs={{0,4},{1,5},{2,6},{3,7},{4,0},{5,1},{6,2},{7,3},{8,12},{9,13},{10,... | collective-permute-start | bytes 2162696 | tf_op jit(solution)/shard_map/ppermute | solution.py:623
  296.3 50.5 %collective-permute-start.21 = (bf16[256,2816]{1,0:T(8,128)(2,1)}, bf16[256,2816]{1,0:T(8,128)(2,1)}, u32[]{:S(2)}, u32[]{:S(2)}) collective-permute-start(bf16[256,2816]{1,0:T(8,128)(2,1)} %get-tuple-element.80), channel_id=1, source_target_pairs={{0,2},{1,3},{2,0},{3,1},{4,6},{5,7},{6,4},{7,5},{8,10},{9,11},{10,... | collective-permute-start | bytes 4325384 | tf_op jit(solution)/shard_map/ppermute | solution.py:623
  298.7 157.2 %all-to-all-start.5 = ((bf16[32,32,1024]{2,1,0:T(8,128)(2,1)}), bf16[32,32,1024]{2,1,0:T(8,128)(2,1)S(1)}, u32[]{:S(2)}, u32[]{:S(2)}) async-start(bf16[32,32,1024]{2,1,0:T(8,128)(2,1)} %after.10), calls=%async_computation.5 | async-start | bytes 4194304 | tf_op jit(solution)/shard_map/all_to_all | solution.py:764
  306.3 10.7 %copy-start.21 = (bf16[128,1024]{1,0:T(8,128)(2,1)S(1)}, bf16[128,1024]{1,0:T(8,128)(2,1)}, u32[]{:S(2)}) copy-start(bf16[128,1024]{1,0:T(8,128)(2,1)} %get-tuple-element.59.mixed_low) | copy-start | bytes 786436
  316.6 6.6 %collective-permute-start.3 = (bf16[128,4224]{1,0:T(8,128)(2,1)}, bf16[128,4224]{1,0:T(8,128)(2,1)S(1)}, u32[]{:S(2)}, u32[]{:S(2)}) collective-permute-start(bf16[128,4224]{1,0:T(8,128)(2,1)} %get-tuple-element.70.refs_6_.refs_10_.refs_2_), channel_id=1, source_target_pairs={{0,1},{1,0},{2,3},{3,2},{4,5},{5,4},{6,7},{7,6},{8,9},{9,8},{10,11... | collective-permute-start | bytes 3244040 | tf_op jit(solution)/shard_map/ppermute | solution.py:623
  319.9 1.4 collective-permute-start.4
  321.3 8.8 %collective-permute-start.5 = (bf16[128,512]{1,0:T(8,128)(2,1)}, bf16[128,512]{1,0:T(8,128)(2,1)S(1)}, u32[]{:S(2)}, u32[]{:S(2)}) collective-permute-start(bf16[128,512]{1,0:T(8,128)(2,1)} %get-tuple-element.120), channel_id=1, source_target_pairs={{0,1},{1,0},{2,3},{3,2},{4,5},{5,4},{6,7},{7,6},{8,9},{9,8},{10,11... | collective-permute-start | bytes 393224 | tf_op jit(solution)/shard_map/ppermute | solution.py:623
  321.5 1.6 collective-permute-start
  323.1 7.0 %collective-permute-start.6 = (bf16[8,512]{1,0:T(8,128)(2,1)S(1)}, bf16[8,512]{1,0:T(8,128)(2,1)S(1)}, u32[]{:S(2)}, u32[]{:S(2)}) collective-permute-start(bf16[8,512]{1,0:T(8,128)(2,1)S(1)} %get-tuple-element.138), channel_id=1, source_target_pairs={{0,1},{1,0},{2,3},{3,2},{4,5},{5,4},{6,7},{7,6},{8,9},{9,8},{10,11... | collective-permute-start | bytes 24584 | tf_op jit(solution)/shard_map/ppermute | solution.py:623
  328.2 84.0 %collective-permute-start.12 = (bf16[256,2048]{1,0:T(8,128)(2,1)}, bf16[256,2048]{1,0:T(8,128)(2,1)}, u32[]{:S(2)}, u32[]{:S(2)}) collective-permute-start(bf16[256,2048]{1,0:T(8,128)(2,1)} %get-tuple-element.78.refs_0_), channel_id=1, source_target_pairs={{0,2},{1,3},{2,0},{3,1},{4,6},{5,7},{6,4},{7,5},{8,10},{9,11},{10,... | collective-permute-start | bytes 3145736 | tf_op jit(solution)/shard_map/ppermute | solution.py:623
  335.2 79.4 %collective-permute-start.7 = (bf16[256,2176]{1,0:T(8,128)(2,1)}, bf16[256,2176]{1,0:T(8,128)(2,1)}, u32[]{:S(2)}, u32[]{:S(2)}) collective-permute-start(bf16[256,2176]{1,0:T(8,128)(2,1)} %get-tuple-element.77), channel_id=1, source_target_pairs={{0,4},{1,5},{2,6},{3,7},{4,0},{5,1},{6,2},{7,3},{8,12},{9,13},{10,... | collective-permute-start | bytes 3342344 | tf_op jit(solution)/shard_map/ppermute | solution.py:623
  336.7 10.1 %copy-start.6 = (bf16[256,2816]{1,0:T(8,128)(2,1)S(1)}, bf16[256,2816]{1,0:T(8,128)(2,1)}, u32[]{:S(2)}) copy-start(bf16[256,2816]{1,0:T(8,128)(2,1)} %after.12) | copy-start | bytes 4325380
  339.1 43.4 %collective-permute-start.28 = (bf16[4,32,1408]{2,1,0:T(8,128)(2,1)S(1)}, bf16[4,32,1408]{2,1,0:T(8,128)(2,1)}, u32[]{:S(2)}, u32[]{:S(2)}) collective-permute-start(bf16[4,32,1408]{2,1,0:T(8,128)(2,1)S(1)} %dynamic-slice_bitcast_fusion.3), channel_id=1, source_target_pairs={{0,2},{1,3},{2,0},{3,1},{4,6},{5,7},{6,4},{7,5},{8,10},{9,11},{10,... | collective-permute-start | bytes 1081352 | tf_op jit(solution)/shard_map/ppermute | solution.py:623
  349.5 38.2 %collective-permute-start.22 = (bf16[4,32,2816]{2,1,0:T(8,128)(2,1)}, bf16[4,32,2816]{2,1,0:T(8,128)(2,1)}, u32[]{:S(2)}, u32[]{:S(2)}) collective-permute-start(bf16[4,32,2816]{2,1,0:T(8,128)(2,1)} %dynamic-slice_bitcast_fusion), channel_id=1, source_target_pairs={{0,4},{1,5},{2,6},{3,7},{4,0},{5,1},{6,2},{7,3},{8,12},{9,13},{10,... | collective-permute-start | bytes 2162696 | tf_op jit(solution)/shard_map/ppermute | solution.py:623
  383.8 5.3 %collective-permute-start.29 = (bf16[32,1408]{1,0:T(8,128)(2,1)S(1)}, bf16[32,1408]{1,0:T(8,128)(2,1)S(1)}, u32[]{:S(2)}, u32[]{:S(2)}) collective-permute-start(bf16[32,1408]{1,0:T(8,128)(2,1)S(1)} %get-tuple-element.109), channel_id=1, source_target_pairs={{0,8},{1,9},{2,10},{3,11},{4,12},{5,13},{6,14},{7,15},{8,0},{9,1},... | collective-permute-start | bytes 270344 | tf_op jit(solution)/shard_map/ppermute | solution.py:623
  385.3 7.2 %collective-permute-start.31 = (bf16[32,1408]{1,0:T(8,128)(2,1)S(1)}, bf16[32,1408]{1,0:T(8,128)(2,1)S(1)}, u32[]{:S(2)}, u32[]{:S(2)}) collective-permute-start(bf16[32,1408]{1,0:T(8,128)(2,1)S(1)} %get-tuple-element.110), channel_id=1, source_target_pairs={{0,24},{1,25},{2,26},{3,27},{4,28},{5,29},{6,30},{7,31},{8,16},{9,... | collective-permute-start | bytes 270344 | tf_op jit(solution)/shard_map/ppermute | solution.py:623
  387.7 10.1 %collective-permute-start.30 = (bf16[32,1408]{1,0:T(8,128)(2,1)S(1)}, bf16[32,1408]{1,0:T(8,128)(2,1)S(1)}, u32[]{:S(2)}, u32[]{:S(2)}) collective-permute-start(bf16[32,1408]{1,0:T(8,128)(2,1)S(1)} %get-tuple-element.111), channel_id=1, source_target_pairs={{0,16},{1,17},{2,18},{3,19},{4,20},{5,21},{6,22},{7,23},{8,24},{9,... | collective-permute-start | bytes 270344 | tf_op jit(solution)/shard_map/ppermute | solution.py:623
  389.1 23.1 %copy-start.2 = (bf16[256,2048]{1,0:T(8,128)(2,1)S(1)}, bf16[256,2048]{1,0:T(8,128)(2,1)}, u32[]{:S(2)}) copy-start(bf16[256,2048]{1,0:T(8,128)(2,1)} %get-tuple-element.71.late) | copy-start | bytes 3145732
  389.2 9.6 %collective-permute-start.23 = (bf16[32,2816]{1,0:T(8,128)(2,1)S(1)}, bf16[32,2816]{1,0:T(8,128)(2,1)S(1)}, u32[]{:S(2)}, u32[]{:S(2)}) collective-permute-start(bf16[32,2816]{1,0:T(8,128)(2,1)S(1)} %get-tuple-element.98), channel_id=1, source_target_pairs={{0,8},{1,9},{2,10},{3,11},{4,12},{5,13},{6,14},{7,15},{8,0},{9,1},... | collective-permute-start | bytes 540680 | tf_op jit(solution)/shard_map/ppermute | solution.py:623
  392.5 10.5 %collective-permute-start.25 = (bf16[32,2816]{1,0:T(8,128)(2,1)S(1)}, bf16[32,2816]{1,0:T(8,128)(2,1)S(1)}, u32[]{:S(2)}, u32[]{:S(2)}) collective-permute-start(bf16[32,2816]{1,0:T(8,128)(2,1)S(1)} %get-tuple-element.99), channel_id=1, source_target_pairs={{0,24},{1,25},{2,26},{3,27},{4,28},{5,29},{6,30},{7,31},{8,16},{9,... | collective-permute-start | bytes 540680 | tf_op jit(solution)/shard_map/ppermute | solution.py:623
  397.8 12.8 %collective-permute-start.24 = (bf16[32,2816]{1,0:T(8,128)(2,1)S(1)}, bf16[32,2816]{1,0:T(8,128)(2,1)S(1)}, u32[]{:S(2)}, u32[]{:S(2)}) collective-permute-start(bf16[32,2816]{1,0:T(8,128)(2,1)S(1)} %get-tuple-element.100), channel_id=1, source_target_pairs={{0,16},{1,17},{2,18},{3,19},{4,20},{5,21},{6,22},{7,23},{8,24},{9,... | collective-permute-start | bytes 540680 | tf_op jit(solution)/shard_map/ppermute | solution.py:623
  414.0 13.2 %collective-permute-start.13 = (bf16[4,32,2048]{2,1,0:T(8,128)(2,1)S(1)}, bf16[4,32,2048]{2,1,0:T(8,128)(2,1)S(1)}, u32[]{:S(2)}, u32[]{:S(2)}) collective-permute-start(bf16[4,32,2048]{2,1,0:T(8,128)(2,1)S(1)} %dynamic-slice_bitcast_fusion.2), channel_id=1, source_target_pairs={{0,4},{1,5},{2,6},{3,7},{4,0},{5,1},{6,2},{7,3},{8,12},{9,13},{10,... | collective-permute-start | bytes 1572872 | tf_op jit(solution)/shard_map/ppermute | solution.py:623
  416.2 14.7 %collective-permute-start.8 = (bf16[4,32,2176]{2,1,0:T(8,128)(2,1)S(1)}, bf16[4,32,2176]{2,1,0:T(8,128)(2,1)S(1)}, u32[]{:S(2)}, u32[]{:S(2)}) collective-permute-start(bf16[4,32,2176]{2,1,0:T(8,128)(2,1)S(1)} %dynamic-slice_bitcast_fusion.1), channel_id=1, source_target_pairs={{0,2},{1,3},{2,0},{3,1},{4,6},{5,7},{6,4},{7,5},{8,10},{9,11},{10,... | collective-permute-start | bytes 1671176 | tf_op jit(solution)/shard_map/ppermute | solution.py:623
  427.4 9.3 %collective-permute-start.14 = (bf16[32,2048]{1,0:T(8,128)(2,1)S(1)}, bf16[32,2048]{1,0:T(8,128)(2,1)S(1)}, u32[]{:S(2)}, u32[]{:S(2)}) collective-permute-start(bf16[32,2048]{1,0:T(8,128)(2,1)S(1)} %get-tuple-element.104), channel_id=1, source_target_pairs={{0,8},{1,9},{2,10},{3,11},{4,12},{5,13},{6,14},{7,15},{8,0},{9,1},... | collective-permute-start | bytes 393224 | tf_op jit(solution)/shard_map/ppermute | solution.py:623
  427.4 9.4 %collective-permute-start.16 = (bf16[32,2048]{1,0:T(8,128)(2,1)S(1)}, bf16[32,2048]{1,0:T(8,128)(2,1)S(1)}, u32[]{:S(2)}, u32[]{:S(2)}) collective-permute-start(bf16[32,2048]{1,0:T(8,128)(2,1)S(1)} %get-tuple-element.105), channel_id=1, source_target_pairs={{0,24},{1,25},{2,26},{3,27},{4,28},{5,29},{6,30},{7,31},{8,16},{9,... | collective-permute-start | bytes 393224 | tf_op jit(solution)/shard_map/ppermute | solution.py:623
  429.1 19.3 %collective-permute-start.15 = (bf16[32,2048]{1,0:T(8,128)(2,1)S(1)}, bf16[32,2048]{1,0:T(8,128)(2,1)S(1)}, u32[]{:S(2)}, u32[]{:S(2)}) collective-permute-start(bf16[32,2048]{1,0:T(8,128)(2,1)S(1)} %get-tuple-element.106), channel_id=1, source_target_pairs={{0,16},{1,17},{2,18},{3,19},{4,20},{5,21},{6,22},{7,23},{8,24},{9,... | collective-permute-start | bytes 393224 | tf_op jit(solution)/shard_map/ppermute | solution.py:623
  431.1 18.8 %collective-permute-start.9 = (bf16[32,2176]{1,0:T(8,128)(2,1)S(1)}, bf16[32,2176]{1,0:T(8,128)(2,1)S(1)}, u32[]{:S(2)}, u32[]{:S(2)}) collective-permute-start(bf16[32,2176]{1,0:T(8,128)(2,1)S(1)} %get-tuple-element.101), channel_id=1, source_target_pairs={{0,8},{1,9},{2,10},{3,11},{4,12},{5,13},{6,14},{7,15},{8,0},{9,1},... | collective-permute-start | bytes 417800 | tf_op jit(solution)/shard_map/ppermute | solution.py:623
  432.1 17.7 %collective-permute-start.11 = (bf16[32,2176]{1,0:T(8,128)(2,1)S(1)}, bf16[32,2176]{1,0:T(8,128)(2,1)S(1)}, u32[]{:S(2)}, u32[]{:S(2)}) collective-permute-start(bf16[32,2176]{1,0:T(8,128)(2,1)S(1)} %get-tuple-element.102), channel_id=1, source_target_pairs={{0,24},{1,25},{2,26},{3,27},{4,28},{5,29},{6,30},{7,31},{8,16},{9,... | collective-permute-start | bytes 417800 | tf_op jit(solution)/shard_map/ppermute | solution.py:623
  436.6 16.2 %collective-permute-start.10 = (bf16[32,2176]{1,0:T(8,128)(2,1)S(1)}, bf16[32,2176]{1,0:T(8,128)(2,1)S(1)}, u32[]{:S(2)}, u32[]{:S(2)}) collective-permute-start(bf16[32,2176]{1,0:T(8,128)(2,1)S(1)} %get-tuple-element.103), channel_id=1, source_target_pairs={{0,16},{1,17},{2,18},{3,19},{4,20},{5,21},{6,22},{7,23},{8,24},{9,... | collective-permute-start | bytes 417800 | tf_op jit(solution)/shard_map/ppermute | solution.py:623
  (26 other events, 76.6 us)
Sparse Core Ops, SparseCore 0:
  13.4 104.3 all-gather.2
  120.6 106.1 all-gather.4
